TPU v7x, 32 devices: a whole 2x2x4 slice. The times are simulated.
32 devices in a mesh: dom: 8 (over z, x), slab: 4 (over y, core).
Axes of the slice: x: 2, y: 2, z: 4, core: 2. Of those that a mesh axis runs over, the one named last changes fastest.
Arguments:
- images: bfloat16 [512, 65536], P(('dom', 'slab')), may hold values from -11 to 11
- references: bfloat16 [16, 65536], P('dom'), may hold values from -6 to 6
- offsets: int32 [512, 2], P(('dom', 'slab')), may hold values from -8 to 8
- orientations: int32 [512, 2], P(('dom', 'slab')), may hold values from 0 to 15, as said below
- interp_mats: bfloat16 [8, 128, 128], replicated, may hold values from -0.5 to 0.5
- interp_index: int32 [512, 2], P(('dom', 'slab')), may hold values from 0 to 7
- owners: int32 [512, 512, 1], P(('dom', 'slab')), may hold values from 0 to 31; in each aligned block of 8192 rows (0 to 8191, 8192 to 16383, ..., all dimensions but the last counted through in order) at most 448 rows name the same one
- line_index: int32 [512, 512], P(('dom', 'slab')), may hold values from 0 to 2047
- volume_in: float32 [65536, 256], P(('dom', 'slab')), may hold values from -6 to 6
Outputs:
- volume: float32 [65536, 256], P(('dom', 'slab'))
- evidence: float32 [512], P(('dom', 'slab'))
Inputs may be any that keep to these rules, and one draw needn't show every extreme that they name: `orientations`: each particle lists 2 different projections. `owners`: among the rows of one device no owner is named more than 448 times, a bound that some block reaches.
All inputs are finite; a program needn't handle non-finite values.
Results may differ from a plain program's by a relative error of at most 0.0039.
Values may be sent and summed in bfloat16 or wider, within the bound.
No kernel may reach another device: no remote copies, remote signals or barrier semaphores. Data moves between devices by JAX's collectives and lax.ppermute only.
A program may use at most 192 MiB of HBM per device.

v0:
```python
import math

import jax
import jax.numpy as jnp
from jax import lax
from jax.sharding import PartitionSpec as P

FY = 256
FX = 128
TX = 4
TY = 4
LIST = 2


def signed_rows(number):
    positions = jnp.arange(number, dtype=jnp.int32)
    return jnp.where(positions >= number // 2, positions - number, positions)


def turn_angle(phase_units, period):
    return 2.0 * math.pi / period * jnp.mod(phase_units, period).astype(jnp.float32)


def grid_tables():
    shift_cols = jnp.arange(TX, dtype=jnp.int32) - TX // 2
    shift_rows = jnp.arange(TY, dtype=jnp.int32) - TY // 2
    col_angle = turn_angle(shift_cols[:, None] * jnp.arange(FX, dtype=jnp.int32)[None, :], FY)
    row_angle = turn_angle(shift_rows[:, None] * signed_rows(FY)[None, :], FY)
    return (jnp.cos(col_angle), jnp.sin(col_angle), jnp.cos(row_angle), jnp.sin(row_angle))


def offset_images(images, offsets):
    number = images.shape[0]
    planes = images.astype(jnp.float32).reshape(number, FY, 2, FX)
    freq_rows = signed_rows(FY)[None, :, None]
    freq_cols = jnp.arange(FX, dtype=jnp.int32)[None, None, :]
    angles = -turn_angle(
        freq_cols * offsets[:, 0][:, None, None] + freq_rows * offsets[:, 1][:, None, None], FY
    )
    cosine = jnp.cos(angles)
    sine_part = jnp.sin(angles)
    real_part = planes[:, :, 0] * cosine - planes[:, :, 1] * sine_part
    imag_part = planes[:, :, 0] * sine_part + planes[:, :, 1] * cosine
    return (real_part, imag_part)


def search_images(real_part, imag_part, row_cos, row_sin):
    number = real_part.shape[0]
    rot_cos = row_cos[None, :, :, None]
    rot_sin = row_sin[None, :, :, None]
    real_new = (real_part[:, None] * rot_cos - imag_part[:, None] * rot_sin).astype(jnp.bfloat16)
    imag_new = (real_part[:, None] * rot_sin + imag_part[:, None] * rot_cos).astype(jnp.bfloat16)
    stacked = jnp.stack([real_new, imag_new], axis=3)
    return stacked.reshape(number * TY, FY * 2 * FX)


def shifted_refs(refs, col_cos, col_sin):
    number = refs.shape[0]
    planes = refs.reshape(number, 1, FY, 2, FX)
    real_in = planes[:, :, :, 0].astype(jnp.float32)
    imag_in = planes[:, :, :, 1].astype(jnp.float32)
    col_cosine = col_cos[None, :, None, :]
    col_sine = col_sin[None, :, None, :]
    real_new = (real_in * col_cosine + imag_in * col_sine).astype(jnp.bfloat16)
    imag_new = (imag_in * col_cosine - real_in * col_sine).astype(jnp.bfloat16)
    stacked = jnp.stack([real_new, imag_new], axis=3)
    return stacked.reshape(number * TX, FY * 2 * FX)


def soft_weights(score_grid, orientations):
    number = score_grid.shape[0]
    flat = score_grid.reshape(number, -1)
    row_max = jnp.max(flat, axis=1)
    evidence = row_max + jnp.log(jnp.sum(jnp.exp(flat - row_max[:, None]), axis=1))
    one_hot_pick = jax.nn.one_hot(orientations, score_grid.shape[2], dtype=jnp.float32)
    picked = jnp.einsum("ilj,ibja->ilba", one_hot_pick, score_grid, precision=lax.Precision.HIGHEST)
    weights = jnp.exp(picked - evidence[:, None, None, None])
    return (evidence, weights)


def weighted_slices(real_part, imag_part, weights, tables):
    col_cos, col_sin, row_cos, row_sin = tables
    high = lax.Precision.HIGHEST
    gate_real = jnp.einsum("ilba,ac->ilbc", weights, col_cos, precision=high)
    gate_imag = jnp.einsum("ilba,ac->ilbc", weights, col_sin, precision=high)
    phase_real = jnp.einsum("br,ilbc->ilrc", row_cos, gate_real, precision=high) - jnp.einsum(
        "br,ilbc->ilrc", row_sin, gate_imag, precision=high
    )
    phase_imag = jnp.einsum("br,ilbc->ilrc", row_cos, gate_imag, precision=high) + jnp.einsum(
        "br,ilbc->ilrc", row_sin, gate_real, precision=high
    )
    image_real = real_part[:, None]
    image_imag = imag_part[:, None]
    slice_real = (image_real * phase_real - image_imag * phase_imag).astype(jnp.bfloat16)
    slice_imag = (image_real * phase_imag + image_imag * phase_real).astype(jnp.bfloat16)
    return jnp.stack([slice_real, slice_imag], axis=3)


def body(
    images,
    references,
    offsets,
    orientations,
    interp_mats,
    interp_index,
    owners,
    line_index,
    volume_in,
):
    number = images.shape[0]
    tables = grid_tables()
    score_scale = 1.0 / math.sqrt(FY * 2 * FX)
    real_part, imag_part = offset_images(images, offsets)
    searched = search_images(real_part, imag_part, tables[2], tables[3])
    total_refs = references.shape[0] * lax.axis_size("dom")
    moved = shifted_refs(
        lax.all_gather(references, "dom", axis=0, tiled=True), tables[0], tables[1]
    )
    block_scores = lax.dot_general(
        searched, moved, (((1,), (1,)), ((), ())), preferred_element_type=jnp.float32
    )
    score_grid = (block_scores * score_scale).reshape(number, TY, total_refs, TX)
    evidence, weights = soft_weights(score_grid, orientations)
    slices = weighted_slices(real_part, imag_part, weights, tables)
    matrices = jnp.take(interp_mats, interp_index, axis=0)
    mixed = jnp.einsum("ilrpc,ilcd->ilrpd", slices, matrices, preferred_element_type=jnp.float32)
    dom_count = lax.axis_size("dom")
    slab_count = lax.axis_size("slab")
    devices = dom_count * slab_count
    per_device = number * LIST * FY
    capacity = max(2, 7 * per_device // (4 * devices))
    flat_rows = mixed.astype(jnp.bfloat16).reshape(per_device, 2 * FX)
    flat_owner = owners.reshape(per_device)
    flat_line = line_index.reshape(per_device)
    owner_match = (flat_owner[:, None] == jnp.arange(devices, dtype=jnp.int32)[None, :]).astype(
        jnp.int32
    )
    running = jnp.cumsum(owner_match, axis=0) - owner_match
    within = jnp.sum(running * owner_match, axis=1)
    slot_index = flat_owner * capacity + within
    send_rows = jnp.zeros((devices * capacity, 2 * FX), jnp.bfloat16).at[slot_index].set(flat_rows)
    send_lines = jnp.zeros((devices * capacity,), jnp.int32).at[slot_index].set(flat_line)
    got_rows, got_lines = (
        lax.all_to_all(
            send_rows.reshape(devices, capacity, 2 * FX),
            ("dom", "slab"),
            split_axis=0,
            concat_axis=0,
            tiled=True,
        ),
        lax.all_to_all(
            send_lines.reshape(devices, capacity),
            ("dom", "slab"),
            split_axis=0,
            concat_axis=0,
            tiled=True,
        ),
    )
    line_count = volume_in.shape[0]
    received_lines = got_lines.reshape(-1)
    received_rows = got_rows.reshape(-1, 2 * FX)
    placing = (jnp.arange(line_count, dtype=jnp.int32)[:, None] == received_lines[None, :]).astype(
        jnp.bfloat16
    )
    added = jnp.dot(placing, received_rows, preferred_element_type=jnp.float32)
    volume = volume_in + added
    return (volume, evidence)


def solution(mesh):
    in_specs = (
        P(("dom", "slab"), None),
        P("dom", None),
        P(("dom", "slab"), None),
        P(("dom", "slab"), None),
        P(),
        P(("dom", "slab"), None),
        P(("dom", "slab"), None, None),
        P(("dom", "slab"), None),
        P(("dom", "slab"), None),
    )
    out_specs = (P(("dom", "slab"), None), P(("dom", "slab")))
    return jax.shard_map(body, mesh=mesh, in_specs=in_specs, out_specs=out_specs, check_vma=False)
```

profile of v0, /device:TPU:0, one launch (start us, length us, event | category | flops | bytes accessed | tf_op | source)
XLA Modules:
  0.0 475.1 jit_solution(5013453428692819386)
XLA Ops:
  9.6 9.5 %reduce-window.6 = s32[32,64,128]{2,1,0:T(8,128)S(1)} reduce-window(s32[32,64,128]{2,1,0:T(8,128)S(1)} %fusion.31, s32[]{:T(128)} %constant.65.clone.1), window={size=1x1x128 pad=0_0x0_0x127_0}, to_apply=%region_0.1 | reduce-window | flops 33292288 | bytes 2097156 | tf_op jit(solution)/shard_map/reduce-window
  21.5 30.5 %scatter_custom_fusion = s32[14336]{0:T(1024)S(1)} fusion(s32[8192]{0:T(1024)S(1)} %bitcast.138, s32[8192]{0:T(1024)S(1)} %bitcast.141, s32[]{:T(128)} %constant.65.clone.1), kind=kCustom, calls=%fused_computation.77 | custom fusion | bytes 57348 | tf_op jit(solution)/shard_map/scatter | solution.py:142
  52.7 7.5 %all-to-all-start = ((s32[32,1,448]{2,1,0:T(1,128)}), s32[32,1,448]{2,1,0:T(1,128)S(1)}, u32[]{:S(2)}, u32[]{:S(2)}) async-start(s32[32,1,448]{2,1,0:T(1,128)} %all_to_all.9), calls=%async_computation | async-start | bytes 131072 | tf_op jit(solution)/shard_map/all_to_all | solution.py:151
  60.3 5.4 %reshape.422 = f32[16,256,2,128]{3,2,1,0:T(2,128)} reshape(bf16[16,65536]{1,0:T(8,128)(2,1)S(1)} %copy-done.3) | data formatting | bytes 6291456 | tf_op jit(solution)/shard_map/reshape | solution.py:34
  65.7 9.0 %fusion.82 = (f32[16,256,1,128]{3,2,1,0:T(1,128)}, f32[16,256,1,128]{3,2,1,0:T(1,128)S(1)}) fusion(f32[16,256,2,128]{3,2,1,0:T(2,128)} %reshape.422), kind=kLoop, calls=%fused_computation.130 | loop fusion | bytes 8388608 | tf_op jit(solution)/shard_map/slice | solution.py:42
  74.7 6.1 %copy.162 = f32[16,256,1,128]{1,3,0,2:T(8,128)} copy(f32[16,256,1,128]{3,2,1,0:T(1,128)} %get-tuple-element.10) | data formatting | bytes 4194304
  80.8 3.6 copy.163
  84.5 11.8 %fusion.22 = (f32[16,256,128]{1,2,0:T(8,128)S(1)}, f32[16,256,128]{1,2,0:T(8,128)}) fusion(f32[16,256,1,128]{1,3,0,2:T(8,128)} %copy.163, f32[16,256,1,128]{1,3,0,2:T(8,128)} %copy.162, s32[16,256]{1,0:T(8,128)S(1)} %broadcast_multiply_fusion.1, s32[16,128]{1,0:T(8,128)S(1)} %iota_multiply_fusion), kind=kLoop, calls=%fused_computation.46 | loop fusion | flops 11010048 | bytes 8413184 | tf_op jit(solution)/shard_map/sub | solution.py:42
  96.4 1.8 copy.135
  98.2 2.9 copy.136
  101.3 6.0 %subtract_convert_fusion.1 = (bf16[16,4,256,1,128]{4,2,3,1,0:T(8,128)(2,1)}, bf16[16,4,256,1,128]{4,2,3,1,0:T(8,128)(2,1)}) fusion(f32[4,256]{1,0:T(4,128)S(1)} %get-tuple-element.15, f32[16,256,128]{2,1,0:T(8,128)} %copy.136, f32[4,256]{1,0:T(4,128)S(1)} %get-tuple-element.14, f32[16,256,128]{2,1,0:T(8,128)} %copy.135), kind=kLoop, calls=%fused_computation.11 | loop fusion | flops 16777216 | bytes 12591104 | tf_op jit(solution)/shard_map/convert_element_type | solution.py:51
  107.3 7.5 %pad_maximum_fusion = bf16[16,4,256,2,128]{4,2,3,1,0:T(8,128)(2,1)} fusion(bf16[16,4,256,1,128]{4,2,3,1,0:T(8,128)(2,1)} %get-tuple-element.7, bf16[16,4,256,1,128]{4,2,3,1,0:T(8,128)(2,1)} %get-tuple-element.6), kind=kLoop, calls=%fused_computation.6 | loop fusion | flops 4194304 | bytes 16777216 | tf_op jit(solution)/shard_map/stack | solution.py:53
  114.7 16.3 %copy.137 = bf16[16,4,256,2,128]{4,3,2,1,0:T(2,128)(2,1)} copy(bf16[16,4,256,2,128]{4,2,3,1,0:T(8,128)(2,1)} %pad_maximum_fusion) | data formatting | bytes 16777216 | tf_op jit(solution)/shard_map/stack | solution.py:53
  131.0 11.4 %reshape.414 = bf16[64,65536]{1,0:T(8,128)(2,1)} reshape(bf16[16,4,256,2,128]{4,3,2,1,0:T(2,128)(2,1)} %copy.137) | data formatting | bytes 16777216 | tf_op jit(solution)/shard_map/reshape | solution.py:54
  142.8 1.7 gather_fusion
  144.7 6.7 %reshape.415 = bf16[16,1,256,2,128]{4,3,2,0,1:T(2,128)(2,1)} reshape(bf16[8,2,65536]{2,1,0:T(2,128)(2,1)} %all-gather.3.cloned.1.call-done) | data formatting | bytes 4194304 | tf_op jit(solution)/shard_map/reshape | solution.py:59
  151.4 6.5 %slice_convert_fusion.1 = (f32[16,1,256,1,128]{4,3,2,0,1:T(1,128)S(1)}, f32[16,1,256,1,128]{4,3,2,0,1:T(1,128)S(1)}) fusion(bf16[16,1,256,2,128]{4,3,2,0,1:T(2,128)(2,1)} %reshape.415), kind=kLoop, calls=%fused_computation.43 | loop fusion | flops 1048576 | bytes 6291456 | tf_op jit(solution)/shard_map/convert_element_type | solution.py:60
  157.8 4.4 add_convert_fusion
  162.2 7.5 %pad_maximum_fusion.1 = bf16[16,4,256,2,128]{4,2,3,1,0:T(8,128)(2,1)} fusion(bf16[16,4,256,1,128]{4,2,3,1,0:T(8,128)(2,1)} %get-tuple-element.9, bf16[16,4,256,1,128]{4,2,3,1,0:T(8,128)(2,1)} %get-tuple-element.8), kind=kLoop, calls=%fused_computation.7 | loop fusion | flops 4194304 | bytes 16777216 | tf_op jit(solution)/shard_map/stack | solution.py:66
  169.6 16.3 %copy.138 = bf16[16,4,256,2,128]{4,3,2,1,0:T(2,128)(2,1)} copy(bf16[16,4,256,2,128]{4,2,3,1,0:T(8,128)(2,1)} %pad_maximum_fusion.1) | data formatting | bytes 16777216 | tf_op jit(solution)/shard_map/stack | solution.py:66
  185.9 11.5 %reshape.416 = bf16[64,65536]{1,0:T(8,128)(2,1)} reshape(bf16[16,4,256,2,128]{4,3,2,1,0:T(2,128)(2,1)} %copy.138) | data formatting | bytes 16777216 | tf_op jit(solution)/shard_map/reshape | solution.py:67
  197.4 8.1 %fusion.83 = (f32[64]{0:T(128)S(1)}, f32[64,64]{0,1:T(8,128)S(1)}) fusion(bf16[64,65536]{1,0:T(8,128)(2,1)} %reshape.414, bf16[64,65536]{1,0:T(8,128)(2,1)} %reshape.416), kind=kOutput, calls=%fused_computation.131 | convolution fusion | flops 536879040 | bytes 16793856 | tf_op jit(solution)/shard_map/dot_general | solution.py:119
  206.5 1.7 copy.151
  209.4 3.6 fusion.38
  212.9 3.6 fusion.34
  216.5 3.8 convolution_add_fusion
  220.4 5.0 %fusion.21 = (bf16[16,2,256,1,128]{2,4,1,0,3:T(8,128)(2,1)S(1)}, bf16[16,2,256,1,128]{2,4,1,0,3:T(8,128)(2,1)S(1)}) fusion(f32[16,2,128,256]{3,2,1,0:T(8,128)S(1)} %convolution_add_fusion, f32[16,256,128]{1,2,0:T(8,128)S(1)} %copy-done.2, f32[16,256,128]{1,2,0:T(8,128)S(1)} %get-tuple-element.4, f32[16,2,128,256]{3,2,1,0:T(8,128)S(1)} %fusion.38, ...), kind=kOutput, calls=%fused_computation.41 | convolution fusion | flops 59783168 | bytes 16843792 | tf_op jit(solution)/shard_map/br,ilbc->ilrc/dot_general | solution.py:86
  227.1 6.4 %copy.149 = bf16[16,2,256,2,128]{4,3,2,1,0:T(2,128)(2,1)} copy(bf16[16,2,256,2,128]{4,2,3,1,0:T(8,128)(2,1)S(1)} %fusion.13) | data formatting | bytes 8388608 | tf_op jit(solution)/shard_map/convert_element_type | solution.py:132
  233.5 40.4 %scatter_custom_fusion.1 = bf16[14336,256]{1,0:T(8,128)(2,1)} fusion(s32[8192]{0:T(1024)S(1)} %bitcast.139, bf16[1024,8,2,128]{3,2,1,0:T(2,128)(2,1)} %bitcast.127, bf16[]{:T(256)} %constant.68.clone.1), kind=kCustom, calls=%fused_computation.12 | custom fusion | bytes 11534338 | tf_op jit(solution)/shard_map/scatter | solution.py:141
  273.9 6.1 %all-to-all-start.1 = ((bf16[32,448,256]{2,1,0:T(8,128)(2,1)}), bf16[32,448,256]{2,1,0:T(8,128)(2,1)}, u32[]{:S(2)}, u32[]{:S(2)}) async-start(bf16[32,448,256]{2,1,0:T(8,128)(2,1)} %bitcast.126), calls=%async_computation.1 | async-start | bytes 14680064 | tf_op jit(solution)/shard_map/all_to_all | solution.py:144
  280.3 162.3 %all-to-all-done.1 = bf16[32,448,256]{2,1,0:T(8,128)(2,1)} async-done(((bf16[32,448,256]{2,1,0:T(8,128)(2,1)}), bf16[32,448,256]{2,1,0:T(8,128)(2,1)}, u32[]{:S(2)}, u32[]{:S(2)}) %all-to-all-start.1) | async-done | bytes 7340064 | tf_op jit(solution)/shard_map/all_to_all | solution.py:144
  442.6 25.2 %fusion.12 = f32[2048,256]{1,0:T(8,128)} fusion(f32[2048,256]{1,0:T(8,128)S(1)} %copy-done.11, bf16[14336,256]{1,0:T(8,128)(2,1)} %bitcast.33, s32[14336]{0:T(1024)S(1)} %eq.75), kind=kOutput, calls=%fused_computation.32 | convolution fusion | flops 15062269952 | bytes 11591680 | tf_op jit(solution)/shard_map/dot_general | solution.py:165
  (67 shorter events, 10.3 us)
Async XLA Ops:
  7.2 135.6 %copy-start = (bf16[8,128,128]{2,1,0:T(8,128)(2,1)S(1)}, bf16[8,128,128]{2,1,0:T(8,128)(2,1)}, u32[]{:S(2)}) copy-start(bf16[8,128,128]{2,1,0:T(8,128)(2,1)} %param.13) | copy-start | bytes 786436
  7.2 13.5 %copy-start.5 = (s32[16,512,1]{1,2,0:T(1,128)S(1)}, s32[16,512,1]{1,2,0:T(1,128)}, u32[]{:S(2)}) copy-start(s32[16,512,1]{1,2,0:T(1,128)} %param.15) | copy-start | bytes 98308
  7.2 13.4 %copy-start.6 = (s32[16,512]{1,0:T(8,128)S(1)}, s32[16,512]{1,0:T(8,128)}, u32[]{:S(2)}) copy-start(s32[16,512]{1,0:T(8,128)} %param.16) | copy-start | bytes 98308
  7.2 137.4 %all-gather.3.cloned.1.call-start = ((), (), s32[]{:S(2)}) async-start(), calls=%async_computation.2 | async-start | bytes 2359296 | tf_op jit(solution)/shard_map/all_gather | solution.py:117
  19.1 41.1 %copy-start.3 = (bf16[16,65536]{1,0:T(8,128)(2,1)S(1)}, bf16[16,65536]{1,0:T(8,128)(2,1)}, u32[]{:S(2)}) copy-start(bf16[16,65536]{1,0:T(8,128)(2,1)} %param.9) | copy-start | bytes 6291460
  52.7 221.2 %all-to-all-start = ((s32[32,1,448]{2,1,0:T(1,128)}), s32[32,1,448]{2,1,0:T(1,128)S(1)}, u32[]{:S(2)}, u32[]{:S(2)}) async-start(s32[32,1,448]{2,1,0:T(1,128)} %all_to_all.9), calls=%async_computation | async-start | bytes 131072 | tf_op jit(solution)/shard_map/all_to_all | solution.py:151
  74.7 9.7 %copy-start.9 = (s32[16,2]{0,1:T(2,128)S(1)}, s32[16,2]{0,1:T(2,128)}, u32[]{:S(2)}) copy-start(s32[16,2]{0,1:T(2,128)} %param.11) | copy-start | bytes 388
  131.0 11.4 %copy-start.8 = (s32[16,2]{0,1:T(2,128)S(1)}, s32[16,2]{0,1:T(2,128)}, u32[]{:S(2)}) copy-start(s32[16,2]{0,1:T(2,128)} %param.12) | copy-start | bytes 388
  131.0 11.5 %copy-start.10 = (s32[16,2]{0,1:T(2,128)S(1)}, s32[16,2]{0,1:T(2,128)}, u32[]{:S(2)}) copy-start(s32[16,2]{0,1:T(2,128)} %param.14) | copy-start | bytes 388
  206.4 10.1 %copy-start.7 = (f32[16]{0:T(128)}, f32[16]{0:T(128)S(1)}, u32[]{:S(2)}) copy-start(f32[16]{0:T(128)S(1)} %log_add_fusion) | copy-start | bytes 196
  216.5 3.8 copy-start.2
  220.4 5.0 %copy-start.4 = (bf16[32,128,128]{2,1,0:T(8,128)(2,1)S(1)}, bf16[32,128,128]{2,1,0:T(8,128)(2,1)}, u32[]{:S(2)}) copy-start(bf16[32,128,128]{2,1,0:T(8,128)(2,1)} %gather_fusion) | copy-start | bytes 3145732
  273.9 168.6 %copy-start.11 = (f32[2048,256]{1,0:T(8,128)S(1)}, f32[2048,256]{1,0:T(8,128)}, u32[]{:S(2)}) copy-start(f32[2048,256]{1,0:T(8,128)} %param.17) | copy-start | bytes 6291460
  273.9 168.6 %all-to-all-start.1 = ((bf16[32,448,256]{2,1,0:T(8,128)(2,1)}), bf16[32,448,256]{2,1,0:T(8,128)(2,1)}, u32[]{:S(2)}, u32[]{:S(2)}) async-start(bf16[32,448,256]{2,1,0:T(8,128)(2,1)} %bitcast.126), calls=%async_computation.1 | async-start | bytes 14680064 | tf_op jit(solution)/shard_map/all_to_all | solution.py:144
  442.6 25.2 %copy-start.1 = (bf16[8,128,128]{2,1,0:T(8,128)(2,1)S(1)}, bf16[8,128,128]{2,1,0:T(8,128)(2,1)}, u32[]{:S(2)}) copy-start(bf16[8,128,128]{2,1,0:T(8,128)(2,1)} %param.13) | copy-start | bytes 786436
Sparse Core Ops, SparseCore 0:
  10.2 52.0 all-gather.2
where the time goes:
time: 480 us; the launch traced here: 475 us
  local copies, waits for them, and re-layouts  175 us (36%)
  waiting for transfers between devices  163 us (34%)
  other arithmetic  57 us (12%)
  matrix products  52 us (11%)
  between operations  14.8 us (3%)
  starting transfers between devices  13.6 us (3%)
    all_to_all x1, waiting for transfers between devices, body(): lax.all_to_all(send_rows.reshape(devices, capacity, 2 * FX), ('dom', 'sla...  162 us
    scatter x1, local copies, waits for them, and re-layouts, body(): jnp.zeros((devices * capacity, 2 * FX), jnp.bfloat16).at[slot_index]  40.4 us
    scatter x1, local copies, waits for them, and re-layouts, body(): jnp.zeros((devices * capacity,), jnp.int32).at[slot_index].set(flat_line)  30.5 us
    dot_general x1, matrix products, body(): added = jnp.dot(placing, received_rows, preferred_element_type=jnp.float32)  25.2 us
    another operation x1, local copies, waits for them, and re-layouts, shifted_refs(): stacked = jnp.stack([real_new, imag_new], axis=3)  16.3 us
    another operation x1, local copies, waits for them, and re-layouts, search_images(): stacked = jnp.stack([real_new, imag_new], axis=3)  16.3 us
    sub x1, other arithmetic, offset_images(): real_part = planes[:, :, 0] * cosine - planes[:, :, 1] * sine_part  11.8 us
    reshape x1, local copies, waits for them, and re-layouts, shifted_refs(): return stacked.reshape(number * TX, FY * 2 * FX)  11.5 us
  transfers between devices with their start and end apart: 3, of which 1 were waited for; matrix products, arithmetic and copies ran while one was open for 54% of the time, Pallas kernels for 0%

commit v1 on v0

v1 whole, which is shorter than its diff:
```python
import functools
import math

import jax
import jax.numpy as jnp
import numpy as np
from jax import lax
from jax.experimental import pallas as pl
from jax.experimental.pallas import tpu as pltpu
from jax.sharding import Mesh
from jax.sharding import PartitionSpec as P

FY = 256
FX = 128
TX = 4
TY = 4
LIST = 2
OFF = 8
INNER = 2
F32 = jnp.float32
BF16 = jnp.bfloat16
I32 = jnp.int32
STEP = 2.0 * math.pi / FY
SHIFTS = OFF + max(TX, TY) // 2
NSHIFT = 24


def vmem_params(mib):
    return pltpu.CompilerParams(vmem_limit_bytes=mib << 20)


def whole(shape):
    return pl.BlockSpec(shape, lambda *_: (0,) * len(shape))


def cost(flops, nbytes):
    return pl.CostEstimate(flops=int(flops), bytes_accessed=int(nbytes), transcendentals=0)


def iota(shape, axis):
    return lax.broadcasted_iota(I32, shape, axis)


def split(value):
    high = value.astype(BF16)
    return high, (value - high.astype(F32)).astype(BF16)


def slot_kernel(dests, cap, me_ref, dest_ref, line_ref, slot_ref, meta_ref, hot_ref):
    blocks = dest_ref.shape[0]
    owner_rows = iota((dests, FY), 0)
    for b in range(blocks):
        hot = owner_rows == dest_ref[b : b + 1, :]
        hot_ref[b * dests : (b + 1) * dests, :] = hot.astype(F32).astype(BF16)
    before = (iota((FY, FY), 0) < iota((FY, FY), 1)).astype(F32).astype(BF16)
    prefix = jnp.dot(hot_ref[...], before, preferred_element_type=F32)
    running = jnp.zeros((dests, 1), F32)
    lane = iota((1, FY), 1).astype(F32)
    ranks = iota((cap, FY), 0)
    total = jnp.zeros((4 * dests, cap), F32)
    for b in range(blocks):
        hot = hot_ref[b * dests : (b + 1) * dests, :].astype(F32)
        part = prefix[b * dests : (b + 1) * dests, :]
        rank = jnp.sum(hot * (part + running), axis=0, keepdims=True)
        running = running + part[:, FY - 1 :] + hot[:, FY - 1 :]
        rank_int = rank.astype(I32)
        slot_ref[b : b + 1, :] = dest_ref[b : b + 1, :] * cap + rank_int
        line = line_ref[b : b + 1, :]
        digits = [
            hot * lane,
            hot * float(b),
            hot * (line & 255).astype(F32),
            hot * ((line >> 8) + 1).astype(F32),
        ]
        left = jnp.concatenate(digits, axis=0).astype(BF16)
        right = (ranks == rank_int).astype(F32).astype(BF16)
        total = total + lax.dot_general(
            left, right, (((1,), (1,)), ((), ())), preferred_element_type=F32
        )
    digit = [total[k * dests : (k + 1) * dests, :].astype(I32) for k in range(4)]
    code = (
        digit[0]
        + digit[1] * FY
        + me_ref[0] * (FY * blocks)
        + (digit[2] + (digit[3] - 1) * 256) * 65536
    )
    meta_ref[...] = jnp.where(digit[3] > 0, code, -1)


def row_slots(me, dest, line, dests, cap):
    blocks = dest.shape[0]
    return pl.pallas_call(
        functools.partial(slot_kernel, dests, cap),
        out_shape=(
            jax.ShapeDtypeStruct((blocks, FY), I32),
            jax.ShapeDtypeStruct((dests, cap), I32),
        ),
        in_specs=[
            pl.BlockSpec(memory_space=pltpu.SMEM),
            pl.BlockSpec(memory_space=pltpu.VMEM),
            pl.BlockSpec(memory_space=pltpu.VMEM),
        ],
        scratch_shapes=[pltpu.VMEM((blocks * dests, FY), BF16)],
        compiler_params=vmem_params(48),
        cost_estimate=cost(2e9, 1e6),
        name="slots",
    )(me, dest, line)


def place_kernel(chunks, slot_ref, image_ref, *refs):
    outs, source, buffer = refs[:chunks], refs[chunks], refs[chunks + 1]
    number, width = image_ref.shape
    slots = buffer.shape[0]
    step = 4096

    def widen(k, carry):
        at = pl.ds(pl.multiple_of(k * step, step), step)
        source[:, at] = image_ref[:, at].astype(F32)
        return carry

    lax.fori_loop(0, width // step, widen, 0)
    fill = slots // 56
    zeros = jnp.zeros((fill, 2 * FX), F32)

    def clear(k, carry):
        buffer[pl.ds(pl.multiple_of(k * fill, fill), fill), :] = zeros
        return carry

    lax.fori_loop(0, 56, clear, 0)

    def place(r, carry):
        at = pl.ds(pl.multiple_of(r * 2 * FX, 2 * FX), 2 * FX)
        for n in range(number):
            row = source[n : n + 1, at]
            for which in range(LIST):
                buffer[pl.ds(slot_ref[n * LIST + which, r], 1), :] = row
        return carry

    lax.fori_loop(0, FY, place, 0)
    rows = slots // chunks
    part = rows // 7
    for k in range(chunks):

        def narrow(i, carry, k=k):
            at = pl.multiple_of(i * part, part)
            outs[k][pl.ds(at, part), :] = buffer[pl.ds(k * rows + at, part), :].astype(BF16)
            return carry

        lax.fori_loop(0, 7, narrow, 0)


def placed_rows(slots, images, chunks, rows):
    number, width = images.shape
    return pl.pallas_call(
        functools.partial(place_kernel, chunks),
        out_shape=[jax.ShapeDtypeStruct((rows, 2 * FX), BF16)] * chunks,
        in_specs=[
            pl.BlockSpec(memory_space=pltpu.SMEM),
            pl.BlockSpec(memory_space=pltpu.VMEM),
        ],
        out_specs=[pl.BlockSpec(memory_space=pltpu.VMEM)] * chunks,
        scratch_shapes=[
            pltpu.VMEM((number, width), F32),
            pltpu.VMEM((chunks * rows, 2 * FX), F32),
        ],
        compiler_params=vmem_params(48),
        cost_estimate=cost(1e6, 30e6),
        name="place",
    )(slots, images)


def rotate(real, imag, cosine, sine):
    return real * cosine - imag * sine, real * sine + imag * cosine


def score_kernel(
    half_ref, turn_ref, image_ref, near_ref, far_ref, offset_ref, orient_ref, interp_ref,
    table_ref, evidence_ref,
):
    number = image_ref.shape[0]
    refs = near_ref.shape[0]
    rows_half = FY // 2
    group = 8
    off_x = offset_ref[:, 0:1]
    off_y = offset_ref[:, 1:2]
    lane = iota((number, FX), 1)

    def wave(units):
        angle = STEP * (units & (FY - 1)).astype(F32)
        return jnp.cos(angle), jnp.sin(angle)

    col_cos, col_sin = wave(-lane * off_x)
    one_cos, one_sin = wave(jnp.broadcast_to(-off_y, (number, FX)))
    ref_lane = iota((1, FX), 1)
    x1_cos, x1_sin = wave(jnp.broadcast_to(ref_lane, (refs, FX)))
    x2_cos, x2_sin = wave(jnp.broadcast_to(2 * ref_lane, (refs, FX)))

    def shifts(real, imag, c1, s1, c2, s2):
        rc, rs, ic, is_ = real * c1, real * s1, imag * c1, imag * s1
        pairs = [
            (real * c2 + imag * s2, imag * c2 - real * s2),
            (rc + is_, ic - rs),
            (real, imag),
            (rc - is_, ic + rs),
        ]
        return pairs

    def stacked(pairs):
        return jnp.concatenate(
            [jnp.concatenate([p.astype(BF16), q.astype(BF16)], axis=1) for p, q in pairs],
            axis=0,
        )

    def run(ref, first, total):
        start_cos, start_sin = wave(-(lane * off_x + first * off_y))

        def block(k, carry):
            total, cosine, sine = carry
            lefts, rights = [], []
            for i in range(group):
                r = first + k * group + i
                at = pl.multiple_of(r * 2 * FX, 2 * FX)
                at_ref = pl.multiple_of((k * group + i) * 2 * FX, 2 * FX)
                real = image_ref[:, pl.ds(at, FX)].astype(F32)
                imag = image_ref[:, pl.ds(at + FX, FX)].astype(F32)
                real, imag = rotate(real, imag, cosine, sine)
                cosine, sine = rotate(cosine, sine, one_cos, one_sin)
                lefts.append(
                    stacked(
                        shifts(
                            real, imag, turn_ref[0, r], turn_ref[1, r], turn_ref[2, r], turn_ref[3, r]
                        )
                    )
                )
                real = ref[:, pl.ds(at_ref, FX)].astype(F32)
                imag = ref[:, pl.ds(at_ref + FX, FX)].astype(F32)
                rights.append(stacked(shifts(real, imag, x1_cos, -x1_sin, x2_cos, -x2_sin)))
            total = total + lax.dot_general(
                jnp.concatenate(lefts, axis=1),
                jnp.concatenate(rights, axis=1),
                (((1,), (1,)), ((), ())),
                preferred_element_type=F32,
            )
            return total, cosine, sine

        total, _, _ = lax.fori_loop(0, rows_half // group, block, (total, start_cos, start_sin))
        return total

    half = half_ref[0]
    total = jnp.zeros((TY * number, TX * refs), F32)
    total = run(near_ref, half * rows_half, total)
    total = run(far_ref, (1 - half) * rows_half, total)
    total = total * (1.0 / math.sqrt(FY * 2 * FX))
    parts = [total[b * number : (b + 1) * number, :] for b in range(TY)]
    top = functools.reduce(jnp.maximum, parts)
    top = jnp.max(top, axis=1, keepdims=True)
    mass = sum(jnp.sum(jnp.exp(part - top), axis=1, keepdims=True) for part in parts)
    evidence = top + jnp.log(mass)
    evidence_ref[...] = jnp.broadcast_to(evidence, (number, FX))
    wide = iota((number, TX * refs), 1)
    slot = iota((number, FX), 1)
    table = jnp.where(slot == 32, off_x.astype(F32), 0.0)
    table = jnp.where(slot == 33, off_y.astype(F32), table)
    for l in range(LIST):
        table = jnp.where(slot == 34 + l, interp_ref[:, l : l + 1].astype(F32), table)
        for b in range(TY):
            weights = jnp.exp(parts[b] - evidence)
            for a in range(TX):
                chosen = wide == a * refs + orient_ref[:, l : l + 1]
                value = jnp.sum(jnp.where(chosen, weights, 0.0), axis=1, keepdims=True)
                table = jnp.where(slot == l * 16 + b * TX + a, value, table)
    table_ref[...] = table


def weights_table(half, images, near, far, offsets, orientations, interp_index):
    number = images.shape[0]
    turn = np.arange(FY) * STEP
    turns = np.stack([np.cos(turn), np.sin(turn), np.cos(2 * turn), np.sin(2 * turn)])
    smem = pl.BlockSpec(memory_space=pltpu.SMEM)
    vmem = pl.BlockSpec(memory_space=pltpu.VMEM)
    return pl.pallas_call(
        score_kernel,
        out_shape=[jax.ShapeDtypeStruct((number, FX), F32)] * 2,
        in_specs=[smem, smem] + [vmem] * 6,
        compiler_params=vmem_params(40),
        cost_estimate=cost(3e9, 5e6),
        name="scores",
    )(
        half, jnp.asarray(turns, F32), images, near, far, offsets, orientations, interp_index
    )


def wave_table():
    shift = np.arange(NSHIFT)[:, None] - SHIFTS
    angle = STEP * ((shift * np.arange(FX)[None, :]) % FY)
    table = np.concatenate(
        [
            np.concatenate([np.cos(angle), np.sin(angle)], axis=1),
            np.concatenate([-np.sin(angle), np.cos(angle)], axis=1),
        ],
        axis=0,
    ).astype(np.float32)
    high = table.astype(jnp.bfloat16)
    low = (table - high.astype(np.float32)).astype(jnp.bfloat16)
    return np.concatenate([high, high, low], axis=0)


def gather_kernel(code_ref, row_ref, table_ref, wave_ref, mats_ref, out_ref, mixed_ref):
    rows = row_ref.shape[0]
    lines = out_ref.shape[0]
    members = table_ref.shape[0]
    count = mats_ref.shape[0]
    size = rows // 7
    per = FY * LIST
    table = table_ref[:, :64]
    table_high, table_low = split(table)
    picks = jnp.concatenate([table_high, table_low], axis=1)

    def block(k, carry):
        at = pl.multiple_of(k * size, size)
        code = code_ref[:, pl.ds(at, size)]
        r = code & (FY - 1)
        which = (code >> 8) & 1
        member = (code >> 9) & (members - 1)
        hot = (iota((members, size), 0) == member).astype(F32).astype(BF16)
        got = lax.dot_general(picks, hot, (((0,), (0,)), ((), ())), preferred_element_type=F32)
        got = got[:64] + got[64:]
        first = which == 0
        weight = jnp.where(first, got[0:16], got[16:32])
        off_x = got[32:33].astype(I32)
        off_y = got[33:34].astype(I32)
        interp = jnp.where(first, got[34:35], got[35:36])
        sub = iota((8, size), 0)
        units = r * ((sub & 3) - TY // 2 - off_y) - jnp.where(sub >= 4, FY // 4, 0)
        wave = jnp.cos(STEP * (units & (FY - 1)).astype(F32))
        gate_real = sum(weight[b * TX : (b + 1) * TX] * wave[b : b + 1] for b in range(TY))
        gate_imag = sum(weight[b * TX : (b + 1) * TX] * wave[4 + b : 5 + b] for b in range(TY))
        spot = iota((NSHIFT, size), 0) + off_x
        coef_real = jnp.zeros((NSHIFT, size), F32)
        coef_imag = jnp.zeros((NSHIFT, size), F32)
        for a in range(TX):
            here = spot == a - TX // 2 + SHIFTS
            coef_real = jnp.where(here, gate_real[a : a + 1], coef_real)
            coef_imag = jnp.where(here, gate_imag[a : a + 1], coef_imag)
        high, low = split(jnp.concatenate([coef_real, coef_imag], axis=0))
        coef = jnp.concatenate([high, low, high], axis=0)
        phase = lax.dot_general(
            coef, wave_ref[...], (((0,), (0,)), ((), ())), preferred_element_type=F32
        )
        values = row_ref[pl.ds(at, size), :].astype(F32)
        real, imag = rotate(values[:, :FX], values[:, FX:], phase[:, :FX], phase[:, FX:])
        slices = jnp.concatenate([real, imag], axis=0).astype(BF16)
        column = jnp.transpose(jnp.broadcast_to(interp, (8, size)))[:, 0:1]
        column = jnp.broadcast_to(column, (size, FX))
        column = jnp.concatenate([column, column], axis=0)
        pieces = [
            jnp.where(column == float(q), slices, jnp.zeros_like(slices)) for q in range(count)
        ]
        mixed = jnp.dot(
            jnp.concatenate(pieces, axis=1),
            mats_ref[...].reshape(count * FX, FX),
            preferred_element_type=F32,
        ).astype(BF16)
        mixed_ref[pl.ds(at, size), :FX] = mixed[:size]
        mixed_ref[pl.ds(at, size), FX:] = mixed[size:]
        return carry

    lax.fori_loop(0, 7, block, 0)
    tile = 256
    line = code_ref[...] >> 16

    def gather(t, carry):
        at = pl.multiple_of(t * tile, tile)
        hot = (iota((tile, rows), 0) + at == line).astype(F32).astype(BF16)
        out_ref[pl.ds(at, tile), :] = jnp.dot(hot, mixed_ref[...], preferred_element_type=F32)
        return carry

    lax.fori_loop(0, lines // tile, gather, 0)


def partial_lines(code, rows, table, mats, lines):
    number = rows.shape[0]
    vmem = pl.BlockSpec(memory_space=pltpu.VMEM)
    return pl.pallas_call(
        gather_kernel,
        out_shape=jax.ShapeDtypeStruct((lines, 2 * FX), F32),
        in_specs=[vmem] * 5,
        scratch_shapes=[pltpu.VMEM((number, 2 * FX), BF16)],
        compiler_params=vmem_params(40),
        cost_estimate=cost(2 * number * 2 * FX * lines + 4e9, 6e6),
        name="lines",
    )(code, rows, table, jnp.asarray(wave_table()), mats)


def block_order(planes):
    return np.array(
        [sorted(range(planes), key=lambda d: (-abs(d - z), -d)) for z in range(planes)], np.int32
    )


def body(
    planes, inner, slab,
    images, references, offsets, orientations, interp_mats, interp_index, owners, line_index, volume_in,
):
    number = images.shape[0]
    lines = volume_in.shape[0]
    group = inner * slab
    devices = planes * group
    rows_all = number * LIST * FY
    cap = max(2, 7 * rows_all // (4 * devices))
    rows = group * cap
    z = lax.axis_index("z")
    member = lax.axis_index("x") * slab + lax.axis_index("slab")
    half = lax.axis_index("slab") % 2

    local = references.shape[0]
    width = references.shape[1]
    mine = lax.dynamic_slice_in_dim(references, half * (width // 2), width // 2, axis=1)
    near = lax.all_to_all(
        jnp.broadcast_to(mine[None], (planes * inner,) + mine.shape), ("z", "x"), 0, 0, tiled=True
    ).reshape(planes * inner * local, width // 2)
    far = lax.ppermute(near, "slab", [(i, i ^ 1) for i in range(slab)])

    order = block_order(planes)
    place_of = np.argsort(order, axis=1).astype(np.int32)
    owner = owners.reshape(number * LIST, FY)
    line = line_index.reshape(number * LIST, FY)
    to_place = jnp.asarray(place_of)[z]
    plane_of = owner // group
    chunk_of = sum(jnp.where(plane_of == k, to_place[k], 0) for k in range(planes))
    dest = chunk_of * group + owner % group
    slots, meta = row_slots(member.reshape(1).astype(I32), dest, line, devices, cap)
    sent = placed_rows(slots, images, planes, rows)
    got_meta = lax.all_to_all(
        meta.reshape(planes, group, cap), ("x", "slab"), 1, 1, tiled=True
    ).reshape(planes, 1, rows)
    got = [
        lax.all_to_all(block.reshape(group, cap, 2 * FX), ("x", "slab"), 0, 0, tiled=True).reshape(
            rows, 2 * FX
        )
        for block in sent
    ]

    table, evidence = weights_table(
        half.reshape(1).astype(I32), images, near, far, offsets, orientations, interp_index
    )
    tables = lax.all_to_all(
        jnp.broadcast_to(table[None], (group,) + table.shape), ("x", "slab"), 0, 0, tiled=True
    ).reshape(group * number, FX)
    parts = [
        partial_lines(got_meta[k], got[k], tables, interp_mats, lines) for k in range(planes)
    ]

    def chosen(index):
        wanted = sorted(set(index.tolist()))
        at = jnp.asarray(index)[z]
        value = parts[wanted[-1]]
        for k in wanted[:-1]:
            value = jnp.where(at == k, parts[k], value)
        return value

    up = down = None
    for s in range(1, planes):
        up_at = np.array([place_of[p, planes - s + p] if p < s else place_of[0, planes - s] for p in range(planes)])
        down_at = np.array(
            [
                place_of[p, p - planes + s] if p >= planes - s else place_of[planes - 1, s - 1]
                for p in range(planes)
            ]
        )
        up_send, down_send = chosen(up_at), chosen(down_at)
        if s > 1:
            up_send = up_send + up.astype(F32)
            down_send = down_send + down.astype(F32)
        up = lax.ppermute(up_send.astype(BF16), "z", [(p, p + 1) for p in range(s)])
        down = lax.ppermute(
            down_send.astype(BF16), "z", [(p, p - 1) for p in range(planes - s, planes)]
        )
    volume = volume_in + parts[planes - 1] + up.astype(F32) + down.astype(F32)
    return volume, evidence[:, 0]


def solution(mesh):
    dom, slab = mesh.shape["dom"], mesh.shape["slab"]
    planes = dom // INNER
    fine = Mesh(mesh.devices.reshape(planes, INNER, slab), ("z", "x", "slab"))
    every = ("z", "x", "slab")
    in_specs = (
        P(every, None),
        P(("z", "x"), None),
        P(every, None),
        P(every, None),
        P(),
        P(every, None),
        P(every, None, None),
        P(every, None),
        P(every, None),
    )
    out_specs = (P(every, None), P(every))
    return jax.shard_map(
        functools.partial(body, planes, INNER, slab),
        mesh=fine,
        in_specs=in_specs,
        out_specs=out_specs,
        check_vma=False,
    )
```

time: 480 us -> 213 us (0.44)
  local copies, waits for them, and re-layouts: 175 us -> 12.8 us
  waiting for transfers between devices: 163 us -> 23.5 us
  Pallas kernels: 0 us -> 103 us
  matrix products: 52 us -> 0 us
  other arithmetic: 57 us -> 15.3 us
  starting transfers between devices: 13.6 us -> 46.7 us
  between operations: 14.8 us -> 2.9 us
  blocking collectives: 0 us -> 7.38 us
    all_to_all x2 -> x6, waiting for transfers between devices: 162 us -> 13.2 us  [the longest x4 8.43 us: body(): lax.all_to_all(block.reshape(group, cap, 2 * FX), ('x', 'slab'), 0, 0, ti...]
    pallas_call x0 -> x7, Pallas kernels: none -> 103 us  [the longest x4 65.2 us: partial_lines(): pl.pallas_call(gather_kernel, out_shape=jax.ShapeDtypeStruct((lines, 2 *...]
    scatter x2 -> x0, local copies, waits for them, and re-layouts: 70.9 us -> none  [the longest x1 40.4 us: body(): jnp.zeros((devices * capacity, 2 * FX), jnp.bfloat16).at[slot_index]]
    dot_general x10 -> x0, matrix products: 52 us -> none  [the longest x1 25.2 us: body(): added = jnp.dot(placing, received_rows, preferred_element_type=jnp.float32)]
    reshape x6 -> x4, local copies, waits for them, and re-layouts: 37 us -> 2.92 us  [the longest x1 1.48 us: body(): near = lax.all_to_all(jnp.broadcast_to(mine[None], (planes * inner,) + mi...]
    another operation x2 -> x0, local copies, waits for them, and re-layouts: 32.5 us -> none  [the longest x1 16.3 us: shifted_refs(): stacked = jnp.stack([real_new, imag_new], axis=3)]
    another operation x5 -> x0, other arithmetic: 25 us -> none
    ppermute x0 -> x7, starting transfers between devices: none -> 19.3 us  [the longest x3 14.3 us: body(): up = lax.ppermute(up_send.astype(BF16), 'z', [(p, p + 1) for p in range(s)])]
  transfers between devices with their start and end apart: 3 -> 13, of which waited for: 1 -> 5; matrix products, arithmetic and copies ran while one was open for 54% -> 6% of each run, Pallas kernels for 0% -> 48%
where the time goes in v1:
time: 213 us; the launch traced here: 212 us
  Pallas kernels  103 us (48%)
  starting transfers between devices  46.7 us (22%)
  waiting for transfers between devices  23.5 us (11%)
  other arithmetic  15.3 us (7%)
  local copies, waits for them, and re-layouts  12.8 us (6%)
  blocking collectives  7.38 us (3%)
  between operations  2.9 us (1%)
    pallas_call x4, Pallas kernels, partial_lines(): pl.pallas_call(gather_kernel, out_shape=jax.ShapeDtypeStruct((lines, 2 *...  65.2 us
    pallas_call x1, Pallas kernels, placed_rows(): pl.pallas_call(functools.partial(place_kernel, chunks), out_shape=[jax.Sh...  25.5 us
    all_to_all x4, starting transfers between devices, body(): lax.all_to_all(block.reshape(group, cap, 2 * FX), ('x', 'slab'), 0, 0, ti...  17.2 us
    ppermute x3, starting transfers between devices, body(): up = lax.ppermute(up_send.astype(BF16), 'z', [(p, p + 1) for p in range(s)])  14.3 us
    pallas_call x1, Pallas kernels, weights_table(): pl.pallas_call(score_kernel, out_shape=[jax.ShapeDtypeStruct((number, FX)...  10.1 us
    convert_element_type x3, other arithmetic, body(): up = lax.ppermute(up_send.astype(BF16), 'z', [(p, p + 1) for p in range(s)])  8.56 us
    all_to_all x4, waiting for transfers between devices, body(): lax.all_to_all(block.reshape(group, cap, 2 * FX), ('x', 'slab'), 0, 0, ti...  8.43 us
    all_to_all x1, blocking collectives, body(): lax.all_to_all(jnp.broadcast_to(table[None], (group,) + table.shape), ('x...  7.38 us
  transfers between devices with their start and end apart: 13, of which 5 were waited for; matrix products, arithmetic and copies ran while one was open for 6% of the time, Pallas kernels for 48%

profile of v1, /device:TPU:0, one launch (start us, length us, event | category | flops | bytes accessed | tf_op | source)
XLA Modules:
  0.0 212.1 jit_solution(16145145548619281323)
XLA Ops:
  3.7 2.6 %fusion.dest_ref = s32[32,256]{1,0:T(8,128)S(1)} fusion(s32[32,256]{1,0:T(8,128)S(1)} %reshape.75, s32[]{:T(128)} %bitcast.4, s32[]{:T(128)} %bitcast.3, s32[]{:T(128)} %bitcast.2, s32[]{:T(128)} %bitcast.1), kind=kLoop, calls=%fused_computation.10 | loop fusion | flops 262144 | bytes 65552 | tf_op jit(solution)/shard_map/add | solution.py:431
  6.3 2.7 %slots.1 = (s32[32,256]{1,0:T(8,128)S(1)}, s32[32,448]{1,0:T(8,128)S(1)}) custom-call(s32[1]{0:T(128)} %bitcast.me_ref, s32[32,256]{1,0:T(8,128)S(1)} %fusion.dest_ref, s32[32,256]{1,0:T(8,128)S(1)} %reshape.76.line_ref), custom_call_target="tpu_custom_call" | custom-call | flops 2000000000 | bytes 1000000 | tf_op jit(solution)/shard_map/slots/pallas_call | solution.py:92
  9.7 5.2 %all-to-all-start = ((s32[4,8,448]{2,0,1:T(4,128)}), s32[4,8,448]{2,0,1:T(4,128)S(1)}, u32[]{:S(2)}, u32[]{:S(2)}) async-start(s32[4,8,448]{2,0,1:T(4,128)} %copy.26), calls=%async_computation | async-start | bytes 131072 | tf_op jit(solution)/shard_map/all_to_all | solution.py:434
  15.0 4.7 %all-to-all-done = s32[4,8,448]{2,0,1:T(4,128)S(1)} async-done(((s32[4,8,448]{2,0,1:T(4,128)}), s32[4,8,448]{2,0,1:T(4,128)S(1)}, u32[]{:S(2)}, u32[]{:S(2)}) %all-to-all-start) | async-done | bytes 57376 | tf_op jit(solution)/shard_map/all_to_all | solution.py:434
  19.7 1.5 broadcast_in_dim.34
  21.2 5.1 %all-to-all-start.2 = ((bf16[8,2,32768]{2,1,0:T(2,128)(2,1)}), bf16[8,2,32768]{2,1,0:T(2,128)(2,1)}, u32[]{:S(2)}, u32[]{:S(2)}) async-start(bf16[8,2,32768]{2,1,0:T(2,128)(2,1)} %broadcast_in_dim.34), calls=%async_computation.2 | async-start | bytes 2097152 | tf_op jit(solution)/shard_map/all_to_all | solution.py:419
  26.3 25.5 %place.1 = (bf16[3584,256]{1,0:T(8,128)(2,1)S(1)}, bf16[3584,256]{1,0:T(8,128)(2,1)S(1)}, bf16[3584,256]{1,0:T(8,128)(2,1)S(1)}, bf16[3584,256]{1,0:T(8,128)(2,1)}) custom-call(s32[32,256]{1,0:T(8,128)S(1)} %get-tuple-element.11.slot_ref, bf16[16,65536]{1,0:T(8,128)(2,1)} %image_ref.3), custom_call_target="tpu_custom_call" | custom-call | flops 1000000 | bytes 30000000 | tf_op jit(solution)/shard_map/place/pallas_call | solution.py:154
  53.0 1.3 copy-done.5
  55.5 4.5 %all-to-all-start.6 = ((bf16[8,448,256]{2,1,0:T(8,128)(2,1)}), bf16[8,448,256]{2,1,0:T(8,128)(2,1)}, u32[]{:S(2)}, u32[]{:S(2)}) async-start(bf16[8,448,256]{2,1,0:T(8,128)(2,1)} %bitcast.22), calls=%async_computation.6 | async-start | bytes 3670016 | tf_op jit(solution)/shard_map/all_to_all | solution.py:438
  60.0 1.5 reshape.81.near_ref
  62.1 2.2 %collective-permute-done.far_ref = bf16[16,32768]{1,0:T(8,128)(2,1)} collective-permute-done((bf16[16,32768]{1,0:T(8,128)(2,1)S(1)}, bf16[16,32768]{1,0:T(8,128)(2,1)}, u32[]{:S(2)}, u32[]{:S(2)}) %collective-permute-start) | collective-permute-done | bytes 1048608 | tf_op jit(solution)/shard_map/ppermute | solution.py:422
  64.3 10.1 %scores.1 = (f32[16,128]{1,0:T(8,128)S(1)}, f32[16,128]{1,0:T(8,128)S(1)}) custom-call(s32[1]{0:T(128)} %bitcast.8.half_ref, f32[4,256]{1,0:T(4,128)S(1)} %copy-done.9, bf16[16,65536]{1,0:T(8,128)(2,1)S(1)} %copy-done.3, bf16[16,32768]{1,0:T(8,128)(2,1)S(1)} %reshape.81.near_ref, bf16[16,32768]{1,0:T(8,128)(2,1)} %collective-permute-done.far_ref, ...), custom_call_target="tpu_custom_call" | custom-call | flops 3000000000 | bytes 5000000 | tf_op jit(solution)/shard_map/scores/pallas_call | solution.py:281
  74.4 8.4 %all-to-all-done.6 = bf16[8,448,256]{2,1,0:T(8,128)(2,1)} async-done(((bf16[8,448,256]{2,1,0:T(8,128)(2,1)}), bf16[8,448,256]{2,1,0:T(8,128)(2,1)}, u32[]{:S(2)}, u32[]{:S(2)}) %all-to-all-start.6) | async-done | bytes 1835040 | tf_op jit(solution)/shard_map/all_to_all | solution.py:438
  82.8 7.4 %all_to_all.35 = f32[8,16,128]{2,1,0:T(8,128)S(1)} all-to-all(f32[8,16,128]{2,1,0:T(8,128)S(1)} %broadcast_in_dim.35), channel_id=1, replica_groups=mesh['z'=4,'x'=2,'slab'=4] {'x','slab'}, dimensions={0} | all-to-all | bytes 131072 | tf_op jit(solution)/shard_map/all_to_all | solution.py:447
  90.2 4.3 %all-to-all-start.4 = ((bf16[8,448,256]{2,1,0:T(8,128)(2,1)}), bf16[8,448,256]{2,1,0:T(8,128)(2,1)}, u32[]{:S(2)}, u32[]{:S(2)}) async-start(bf16[8,448,256]{2,1,0:T(8,128)(2,1)} %bitcast.20), calls=%async_computation.4 | async-start | bytes 3670016 | tf_op jit(solution)/shard_map/all_to_all | solution.py:438
  94.8 16.6 %lines.7 = f32[2048,256]{1,0:T(8,128)S(1)} custom-call(s32[1,3584]{1,0:T(1,128)S(1)} %squeeze.38.code_ref, bf16[3584,256]{1,0:T(8,128)(2,1)} %bitcast.17.row_ref, f32[128,128]{1,0:T(8,128)S(1)} %bitcast.23, bf16[144,256]{1,0:T(8,128)(2,1)S(1)} %copy-done.8, bf16[8,128,128]{2,1,0:T(8,128)(2,1)S(1)} %copy-done.7), custom_call_target="tpu_custom_call" | custom-call | flops 7758096384 | bytes 6000000 | tf_op jit(solution)/shard_map/lines/pallas_call | solution.py:384
  112.6 5.0 %collective-permute-start.1 = (bf16[2048,256]{1,0:T(8,128)(2,1)}, bf16[2048,256]{1,0:T(8,128)(2,1)}, u32[]{:S(2)}, u32[]{:S(2)}) collective-permute-start(bf16[2048,256]{1,0:T(8,128)(2,1)} %convert_element_type.34), channel_id=1, source_target_pairs={{0,8},{1,9},{2,10},{3,11},{4,12},{5,13},{6,14},{7,15}} | collective-permute-start | bytes 3145736 | tf_op jit(solution)/shard_map/ppermute | solution.py:475
  117.6 1.6 collective-permute-start.4
  121.8 4.3 %all-to-all-start.5 = ((bf16[8,448,256]{2,1,0:T(8,128)(2,1)}), bf16[8,448,256]{2,1,0:T(8,128)(2,1)}, u32[]{:S(2)}, u32[]{:S(2)}) async-start(bf16[8,448,256]{2,1,0:T(8,128)(2,1)} %bitcast.19), calls=%async_computation.5 | async-start | bytes 3670016 | tf_op jit(solution)/shard_map/all_to_all | solution.py:438
  126.1 16.6 %lines.5 = f32[2048,256]{1,0:T(8,128)S(1)} custom-call(s32[1,3584]{1,0:T(1,128)S(1)} %squeeze.36.code_ref, bf16[3584,256]{1,0:T(8,128)(2,1)} %bitcast.12.row_ref, f32[128,128]{1,0:T(8,128)S(1)} %bitcast.24, bf16[144,256]{1,0:T(8,128)(2,1)S(1)} %copy-done.8, bf16[8,128,128]{2,1,0:T(8,128)(2,1)S(1)} %copy-done.7), custom_call_target="tpu_custom_call" | custom-call | flops 7758096384 | bytes 6000000 | tf_op jit(solution)/shard_map/lines/pallas_call | solution.py:384
  142.8 4.1 %add_convert_fusion.3 = (bf16[2048,256]{1,0:T(8,128)(2,1)}, bf16[2048,256]{1,0:T(8,128)(2,1)}) fusion(bf16[2048,256]{1,0:T(8,128)(2,1)} %collective-permute-done.1, f32[2048,256]{1,0:T(8,128)S(1)} %lines.7, f32[2048,256]{1,0:T(8,128)S(1)} %lines.5, pred[]{:T(512)} %bitcast.15, bf16[2048,256]{1,0:T(8,128)(2,1)} %collective-permute-done.4, pred[]{:T(512)} %bitcast.18), kind=kLoop, calls=%fused_computation.4 | loop fusion | flops 4194304 | bytes 8388610 | tf_op jit(solution)/shard_map/convert_element_type | solution.py:475
  147.0 2.4 %collective-permute-start.2 = (bf16[2048,256]{1,0:T(8,128)(2,1)}, bf16[2048,256]{1,0:T(8,128)(2,1)}, u32[]{:S(2)}, u32[]{:S(2)}) collective-permute-start(bf16[2048,256]{1,0:T(8,128)(2,1)} %get-tuple-element.22), channel_id=1, source_target_pairs={{0,8},{8,16},{1,9},{9,17},{2,10},{10,18},{3,11},{11,19},{4,12},{12... | collective-permute-start | bytes 3145736 | tf_op jit(solution)/shard_map/ppermute | solution.py:475
  149.4 1.6 collective-permute-start.5
  152.3 4.1 %all-to-all-start.1 = ((bf16[8,448,256]{2,1,0:T(8,128)(2,1)}), bf16[8,448,256]{2,1,0:T(8,128)(2,1)S(1)}, u32[]{:S(2)}, u32[]{:S(2)}) async-start(bf16[8,448,256]{2,1,0:T(8,128)(2,1)} %bitcast.28), calls=%async_computation.1 | async-start | bytes 3670016 | tf_op jit(solution)/shard_map/all_to_all | solution.py:438
  156.5 16.8 %lines.6 = f32[2048,256]{1,0:T(8,128)S(1)} custom-call(s32[1,3584]{1,0:T(1,128)S(1)} %squeeze.37.code_ref, bf16[3584,256]{1,0:T(8,128)(2,1)} %bitcast.14.row_ref, f32[128,128]{1,0:T(8,128)S(1)} %bitcast.25, bf16[144,256]{1,0:T(8,128)(2,1)S(1)} %copy-done.8, bf16[8,128,128]{2,1,0:T(8,128)(2,1)S(1)} %copy-done.7), custom_call_target="tpu_custom_call" | custom-call | flops 7758096384 | bytes 6000000 | tf_op jit(solution)/shard_map/lines/pallas_call | solution.py:384
  173.3 3.3 %add_convert_fusion.2 = (bf16[2048,256]{1,0:T(8,128)(2,1)}, bf16[2048,256]{1,0:T(8,128)(2,1)}) fusion(bf16[2048,256]{1,0:T(8,128)(2,1)} %collective-permute-done.2, f32[2048,256]{1,0:T(8,128)S(1)} %copy-done.2, f32[2048,256]{1,0:T(8,128)S(1)} %lines.6, pred[]{:T(512)} %bitcast.10, bf16[2048,256]{1,0:T(8,128)(2,1)} %collective-permute-done.5), kind=kLoop, calls=%fused_computation.3 | loop fusion | flops 3670016 | bytes 8388609 | tf_op jit(solution)/shard_map/convert_element_type | solution.py:475
  176.6 6.9 %collective-permute-start.3 = (bf16[2048,256]{1,0:T(8,128)(2,1)}, bf16[2048,256]{1,0:T(8,128)(2,1)}, u32[]{:S(2)}, u32[]{:S(2)}) collective-permute-start(bf16[2048,256]{1,0:T(8,128)(2,1)} %get-tuple-element.24), channel_id=1, source_target_pairs={{0,8},{8,16},{16,24},{1,9},{9,17},{17,25},{2,10},{10,18},{18,26},{... | collective-permute-start | bytes 3145736 | tf_op jit(solution)/shard_map/ppermute | solution.py:475
  183.5 1.3 collective-permute-start.6
  185.5 15.1 %lines.4 = f32[2048,256]{1,0:T(8,128)S(1)} custom-call(s32[1,3584]{1,0:T(1,128)S(1)} %squeeze.35.code_ref, bf16[3584,256]{1,0:T(8,128)(2,1)S(1)} %bitcast.21, f32[128,128]{1,0:T(8,128)S(1)} %bitcast.26, bf16[144,256]{1,0:T(8,128)(2,1)S(1)} %copy-done.8, bf16[8,128,128]{2,1,0:T(8,128)(2,1)S(1)} %copy-done.7), custom_call_target="tpu_custom_call" | custom-call | flops 7758096384 | bytes 6000000 | tf_op jit(solution)/shard_map/lines/pallas_call | solution.py:384
  200.7 3.1 %collective-permute-done.3 = bf16[2048,256]{1,0:T(8,128)(2,1)} collective-permute-done((bf16[2048,256]{1,0:T(8,128)(2,1)}, bf16[2048,256]{1,0:T(8,128)(2,1)}, u32[]{:S(2)}, u32[]{:S(2)}) %collective-permute-start.3) | collective-permute-done | bytes 1048608 | tf_op jit(solution)/shard_map/ppermute | solution.py:475
  203.8 5.1 %collective-permute-done.6 = bf16[2048,256]{1,0:T(8,128)(2,1)} collective-permute-done((bf16[2048,256]{1,0:T(8,128)(2,1)}, bf16[2048,256]{1,0:T(8,128)(2,1)}, u32[]{:S(2)}, u32[]{:S(2)}) %collective-permute-start.6) | collective-permute-done | bytes 1048608 | tf_op jit(solution)/shard_map/ppermute | solution.py:476
  208.9 3.3 %convert_add_fusion = f32[2048,256]{1,0:T(8,128)} fusion(bf16[2048,256]{1,0:T(8,128)(2,1)} %collective-permute-done.6, bf16[2048,256]{1,0:T(8,128)(2,1)} %collective-permute-done.3, f32[2048,256]{1,0:T(8,128)S(1)} %copy-done.10, f32[2048,256]{1,0:T(8,128)S(1)} %lines.4), kind=kLoop, calls=%fused_computation | loop fusion | flops 2621440 | bytes 8388608 | tf_op jit(solution)/shard_map/add | solution.py:479
  (63 shorter events, 11.0 us)
Async XLA Ops:
  0.6 14.2 %copy-start = (bf16[2,65536]{1,0:T(2,128)(2,1)S(1)}, bf16[2,65536]{1,0:T(2,128)(2,1)}, u32[]{:S(2)}) copy-start(bf16[2,65536]{1,0:T(2,128)(2,1)} %param.19) | copy-start | bytes 786436
  9.7 10.0 %all-to-all-start = ((s32[4,8,448]{2,0,1:T(4,128)}), s32[4,8,448]{2,0,1:T(4,128)S(1)}, u32[]{:S(2)}, u32[]{:S(2)}) async-start(s32[4,8,448]{2,0,1:T(4,128)} %copy.26), calls=%async_computation | async-start | bytes 131072 | tf_op jit(solution)/shard_map/all_to_all | solution.py:434
  21.2 34.2 %all-to-all-start.2 = ((bf16[8,2,32768]{2,1,0:T(2,128)(2,1)}), bf16[8,2,32768]{2,1,0:T(2,128)(2,1)}, u32[]{:S(2)}, u32[]{:S(2)}) async-start(bf16[8,2,32768]{2,1,0:T(2,128)(2,1)} %broadcast_in_dim.34), calls=%async_computation.2 | async-start | bytes 2097152 | tf_op jit(solution)/shard_map/all_to_all | solution.py:419
  51.7 1.2 copy-start.4
  53.0 1.3 copy-start.5
  54.2 1.2 copy-start.6
  55.5 6.4 %copy-start.11 = (s32[16,2]{0,1:T(2,128)S(1)}, s32[16,2]{0,1:T(2,128)}, u32[]{:S(2)}) copy-start(s32[16,2]{0,1:T(2,128)} %param.20) | copy-start | bytes 388
  55.5 6.5 %copy-start.12 = (s32[16,2]{0,1:T(2,128)S(1)}, s32[16,2]{0,1:T(2,128)}, u32[]{:S(2)}) copy-start(s32[16,2]{0,1:T(2,128)} %param.21) | copy-start | bytes 388
  55.5 6.6 %copy-start.13 = (s32[16,2]{0,1:T(2,128)S(1)}, s32[16,2]{0,1:T(2,128)}, u32[]{:S(2)}) copy-start(s32[16,2]{0,1:T(2,128)} %param.23) | copy-start | bytes 388
  55.5 8.8 %copy-start.3 = (bf16[16,65536]{1,0:T(8,128)(2,1)S(1)}, bf16[16,65536]{1,0:T(8,128)(2,1)}, u32[]{:S(2)}) copy-start(bf16[16,65536]{1,0:T(8,128)(2,1)} %image_ref.3) | copy-start | bytes 6291460
  55.5 8.8 %copy-start.9 = (f32[4,256]{1,0:T(4,128)S(1)}, f32[4,256]{1,0:T(4,128)}, u32[]{:S(2)}) copy-start(f32[4,256]{1,0:T(4,128)} %constant.82.clone.turn_ref) | copy-start | bytes 12292
  55.5 27.3 %all-to-all-start.6 = ((bf16[8,448,256]{2,1,0:T(8,128)(2,1)}), bf16[8,448,256]{2,1,0:T(8,128)(2,1)}, u32[]{:S(2)}, u32[]{:S(2)}) async-start(bf16[8,448,256]{2,1,0:T(8,128)(2,1)} %bitcast.22), calls=%async_computation.6 | async-start | bytes 3670016 | tf_op jit(solution)/shard_map/all_to_all | solution.py:438
  61.4 2.9 %collective-permute-start = (bf16[16,32768]{1,0:T(8,128)(2,1)S(1)}, bf16[16,32768]{1,0:T(8,128)(2,1)}, u32[]{:S(2)}, u32[]{:S(2)}) collective-permute-start(bf16[16,32768]{1,0:T(8,128)(2,1)S(1)} %reshape.81.near_ref), channel_id=1, source_target_pairs={{0,1},{1,0},{2,3},{3,2},{4,5},{5,4},{6,7},{7,6},{8,9},{9,8},{10,11... | collective-permute-start | bytes 3145736 | tf_op jit(solution)/shard_map/ppermute | solution.py:422
  74.4 20.4 %copy-start.7 = (bf16[8,128,128]{2,1,0:T(8,128)(2,1)S(1)}, bf16[8,128,128]{2,1,0:T(8,128)(2,1)}, u32[]{:S(2)}) copy-start(bf16[8,128,128]{2,1,0:T(8,128)(2,1)} %mats_ref.7) | copy-start | bytes 786436
  74.4 20.4 %copy-start.8 = (bf16[144,256]{1,0:T(8,128)(2,1)S(1)}, bf16[144,256]{1,0:T(8,128)(2,1)}, u32[]{:S(2)}) copy-start(bf16[144,256]{1,0:T(8,128)(2,1)} %constant.83.clone.wave_ref) | copy-start | bytes 221188
  90.2 31.6 %all-to-all-start.4 = ((bf16[8,448,256]{2,1,0:T(8,128)(2,1)}), bf16[8,448,256]{2,1,0:T(8,128)(2,1)}, u32[]{:S(2)}, u32[]{:S(2)}) async-start(bf16[8,448,256]{2,1,0:T(8,128)(2,1)} %bitcast.20), calls=%async_computation.4 | async-start | bytes 3670016 | tf_op jit(solution)/shard_map/all_to_all | solution.py:438
  111.5 7.8 %copy-start.16 = (s32[4]{0:T(128)S(1)}, s32[4]{0:T(128)}, u32[]{:S(2)}) copy-start(s32[4]{0:T(128)} %constant.84.clone) | copy-start | bytes 52
  111.5 8.4 %copy-start.15 = (s32[4]{0:T(128)S(1)}, s32[4]{0:T(128)}, u32[]{:S(2)}) copy-start(s32[4]{0:T(128)} %constant.85.clone) | copy-start | bytes 52
  112.6 30.2 %collective-permute-start.1 = (bf16[2048,256]{1,0:T(8,128)(2,1)}, bf16[2048,256]{1,0:T(8,128)(2,1)}, u32[]{:S(2)}, u32[]{:S(2)}) collective-permute-start(bf16[2048,256]{1,0:T(8,128)(2,1)} %convert_element_type.34), channel_id=1, source_target_pairs={{0,8},{1,9},{2,10},{3,11},{4,12},{5,13},{6,14},{7,15}} | collective-permute-start | bytes 3145736 | tf_op jit(solution)/shard_map/ppermute | solution.py:475
  117.6 25.2 %collective-permute-start.4 = (bf16[2048,256]{1,0:T(8,128)(2,1)}, bf16[2048,256]{1,0:T(8,128)(2,1)}, u32[]{:S(2)}, u32[]{:S(2)}) collective-permute-start(bf16[2048,256]{1,0:T(8,128)(2,1)} %convert_element_type.34), channel_id=1, source_target_pairs={{24,16},{25,17},{26,18},{27,19},{28,20},{29,21},{30,22},{31,23}} | collective-permute-start | bytes 3145736 | tf_op jit(solution)/shard_map/ppermute | solution.py:476
  121.8 30.5 %all-to-all-start.5 = ((bf16[8,448,256]{2,1,0:T(8,128)(2,1)}), bf16[8,448,256]{2,1,0:T(8,128)(2,1)}, u32[]{:S(2)}, u32[]{:S(2)}) async-start(bf16[8,448,256]{2,1,0:T(8,128)(2,1)} %bitcast.19), calls=%async_computation.5 | async-start | bytes 3670016 | tf_op jit(solution)/shard_map/all_to_all | solution.py:438
  142.8 4.2 %copy-start.1 = (f32[2048,256]{1,0:T(8,128)}, f32[2048,256]{1,0:T(8,128)S(1)}, u32[]{:S(2)}) copy-start(f32[2048,256]{1,0:T(8,128)S(1)} %lines.5) | copy-start | bytes 6291460
  142.8 8.2 %copy-start.14 = (s32[4]{0:T(128)S(1)}, s32[4]{0:T(128)}, u32[]{:S(2)}) copy-start(s32[4]{0:T(128)} %constant.86.clone) | copy-start | bytes 52
  147.0 26.3 %collective-permute-start.2 = (bf16[2048,256]{1,0:T(8,128)(2,1)}, bf16[2048,256]{1,0:T(8,128)(2,1)}, u32[]{:S(2)}, u32[]{:S(2)}) collective-permute-start(bf16[2048,256]{1,0:T(8,128)(2,1)} %get-tuple-element.22), channel_id=1, source_target_pairs={{0,8},{8,16},{1,9},{9,17},{2,10},{10,18},{3,11},{11,19},{4,12},{12... | collective-permute-start | bytes 3145736 | tf_op jit(solution)/shard_map/ppermute | solution.py:475
  149.4 23.9 %collective-permute-start.5 = (bf16[2048,256]{1,0:T(8,128)(2,1)}, bf16[2048,256]{1,0:T(8,128)(2,1)}, u32[]{:S(2)}, u32[]{:S(2)}) collective-permute-start(bf16[2048,256]{1,0:T(8,128)(2,1)} %get-tuple-element.23), channel_id=1, source_target_pairs={{16,8},{24,16},{17,9},{25,17},{18,10},{26,18},{19,11},{27,19},{20,... | collective-permute-start | bytes 3145736 | tf_op jit(solution)/shard_map/ppermute | solution.py:476
  152.3 33.2 %all-to-all-start.1 = ((bf16[8,448,256]{2,1,0:T(8,128)(2,1)}), bf16[8,448,256]{2,1,0:T(8,128)(2,1)S(1)}, u32[]{:S(2)}, u32[]{:S(2)}) async-start(bf16[8,448,256]{2,1,0:T(8,128)(2,1)} %bitcast.28), calls=%async_computation.1 | async-start | bytes 3670016 | tf_op jit(solution)/shard_map/all_to_all | solution.py:438
  156.4 16.8 %copy-start.2 = (f32[2048,256]{1,0:T(8,128)S(1)}, f32[2048,256]{1,0:T(8,128)}, u32[]{:S(2)}) copy-start(f32[2048,256]{1,0:T(8,128)} %copy-done.1) | copy-start | bytes 6291460
  176.6 27.2 %collective-permute-start.3 = (bf16[2048,256]{1,0:T(8,128)(2,1)}, bf16[2048,256]{1,0:T(8,128)(2,1)}, u32[]{:S(2)}, u32[]{:S(2)}) collective-permute-start(bf16[2048,256]{1,0:T(8,128)(2,1)} %get-tuple-element.24), channel_id=1, source_target_pairs={{0,8},{8,16},{16,24},{1,9},{9,17},{17,25},{2,10},{10,18},{18,26},{... | collective-permute-start | bytes 3145736 | tf_op jit(solution)/shard_map/ppermute | solution.py:475
  183.5 25.3 %collective-permute-start.6 = (bf16[2048,256]{1,0:T(8,128)(2,1)}, bf16[2048,256]{1,0:T(8,128)(2,1)}, u32[]{:S(2)}, u32[]{:S(2)}) collective-permute-start(bf16[2048,256]{1,0:T(8,128)(2,1)} %get-tuple-element.25), channel_id=1, source_target_pairs={{8,0},{16,8},{24,16},{9,1},{17,9},{25,17},{10,2},{18,10},{26,18},{... | collective-permute-start | bytes 3145736 | tf_op jit(solution)/shard_map/ppermute | solution.py:476
  185.5 23.3 %copy-start.10 = (f32[2048,256]{1,0:T(8,128)S(1)}, f32[2048,256]{1,0:T(8,128)}, u32[]{:S(2)}) copy-start(f32[2048,256]{1,0:T(8,128)} %param.26) | copy-start | bytes 6291460

commit v2 on v1

v2 whole, which is shorter than its diff:
```python
import functools
import math

import jax
import jax.numpy as jnp
import numpy as np
from jax import lax
from jax.experimental import pallas as pl
from jax.experimental.pallas import tpu as pltpu
from jax.sharding import Mesh
from jax.sharding import PartitionSpec as P

FY = 256
FX = 128
TX = 4
TY = 4
LIST = 2
OFF = 8
INNER = 2
F32 = jnp.float32
BF16 = jnp.bfloat16
I32 = jnp.int32
STEP = 2.0 * math.pi / FY
SHIFTS = OFF + max(TX, TY) // 2
NSHIFT = 24


def vmem_params(mib):
    return pltpu.CompilerParams(vmem_limit_bytes=mib << 20)


def whole(shape):
    return pl.BlockSpec(shape, lambda *_: (0,) * len(shape))


def cost(flops, nbytes):
    return pl.CostEstimate(flops=int(flops), bytes_accessed=int(nbytes), transcendentals=0)


def iota(shape, axis):
    return lax.broadcasted_iota(I32, shape, axis)


def split(value):
    high = value.astype(BF16)
    return high, (value - high.astype(F32)).astype(BF16)


def slot_kernel(
    dests, group, pad, place_ref, owner_ref, line_ref, image_ref,
    index_ref, digit_ref, real_ref, imag_ref, hot_ref,
):
    number = owner_ref.shape[0]
    blocks = number * LIST
    planes = dests // group
    z = lax.axis_index("z")

    def widen(k, carry):
        for i in range(8):
            r = k * 8 + i
            at = pl.multiple_of(r * 2 * FX, 2 * FX)
            to = pl.ds(pl.multiple_of(r * number, number), number)
            real_ref[to, :] = image_ref[:, pl.ds(at, FX)].astype(F32)
            imag_ref[to, :] = image_ref[:, pl.ds(at + FX, FX)].astype(F32)
        return carry

    lax.fori_loop(0, FY // 8, widen, 0)
    owner = owner_ref[...]
    plane = owner // group
    chunk = jnp.zeros_like(owner)
    for k in range(planes):
        chunk = jnp.where(plane == k, place_ref[z, k], chunk)
    dest = chunk * group + (owner & (group - 1))
    owner_rows = iota((dests, FY), 0)
    for b in range(blocks):
        n, l = b // LIST, b % LIST
        hot = owner_rows == dest[n : n + 1, l * FY : (l + 1) * FY]
        hot_ref[b * dests : (b + 1) * dests, :] = hot.astype(F32).astype(BF16)
    before = (iota((FY, FY), 0) < iota((FY, FY), 1)).astype(F32).astype(BF16)
    prefix = jnp.dot(hot_ref[...], before, preferred_element_type=F32)
    running = jnp.zeros((dests, 1), F32)
    lane = iota((1, FY), 1).astype(F32)
    ranks = iota((pad, FY), 0)
    total = jnp.zeros((4 * dests, pad), F32)
    for b in range(blocks):
        n, l = b // LIST, b % LIST
        hot = hot_ref[b * dests : (b + 1) * dests, :].astype(F32)
        part = prefix[b * dests : (b + 1) * dests, :]
        rank = jnp.sum(hot * (part + running), axis=0, keepdims=True).astype(I32)
        running = running + part[:, FY - 1 :] + hot[:, FY - 1 :]
        line = line_ref[n : n + 1, l * FY : (l + 1) * FY]
        digits = [
            hot * lane,
            hot * float(b),
            hot * (line & 255).astype(F32),
            hot * ((line >> 8) + 1).astype(F32),
        ]
        left = jnp.concatenate(digits, axis=0).astype(BF16)
        right = (ranks == rank).astype(F32).astype(BF16)
        total = total + lax.dot_general(
            left, right, (((1,), (1,)), ((), ())), preferred_element_type=F32
        )
    digit_ref[...] = total
    row = total[:dests].astype(I32) * number + (total[dests : 2 * dests].astype(I32) >> 1)
    index_ref[...] = jnp.where(iota((dests, pad), 1) == pad - 1, running.astype(I32), row)


def row_slots(places, owners, lines, images, dests, group, pad):
    number, width = images.shape
    return pl.pallas_call(
        functools.partial(slot_kernel, dests, group, pad),
        out_shape=(
            jax.ShapeDtypeStruct((dests, pad), I32),
            jax.ShapeDtypeStruct((4 * dests, pad), F32),
            pltpu.VMEM((number * FY, FX), F32),
            pltpu.VMEM((number * FY, FX), F32),
        ),
        in_specs=[pl.BlockSpec(memory_space=pltpu.SMEM)]
        + [pl.BlockSpec(memory_space=pltpu.VMEM)] * 3,
        scratch_shapes=[pltpu.VMEM((number * LIST * dests, FY), BF16)],
        compiler_params=vmem_params(24),
        cost_estimate=cost(3e9, 12e6),
        name="slots",
    )(places, owners, lines, images)


def place_kernel(
    chunk, cap, index_ref, digit_ref, real_ref, imag_ref, out_ref, left_ref, right_ref, held, sems
):
    group, pad = index_ref.shape
    dests = digit_ref.shape[0] // 4
    words = pad // (2 * FX)
    span = cap + 16
    zeros = jnp.zeros((group * span, FX), F32)

    left_ref[...] = zeros
    right_ref[...] = zeros
    copies = []
    for d in range(group):
        start = d * span

        def eight(i, inner, d=d, start=start):
            for j in range(8):
                w = i * 8 + j
                at = index_ref[d, w]
                left_ref[pl.ds(start + w, 1), :] = real_ref[pl.ds(at, 1), :]
                right_ref[pl.ds(start + w, 1), :] = imag_ref[pl.ds(at, 1), :]
            return inner

        lax.fori_loop(0, (index_ref[d, pad - 1] + 7) // 8, eight, 0)
        for which in range(4):
            row = which * dests + chunk * group + d
            for word in range(words):
                to = start + cap + which * words + word
                lane = word * 2 * FX
                left_ref[to : to + 1, :] = digit_ref[row : row + 1, lane : lane + FX]
                right_ref[to : to + 1, :] = digit_ref[row : row + 1, lane + FX : lane + 2 * FX]
        at = slice(start, start + span)
        held[at, :FX] = left_ref[at, :].astype(BF16)
        held[at, FX:] = right_ref[at, :].astype(BF16)
        copies.append(pltpu.make_async_copy(held.at[at], out_ref.at[at], sems.at[d]))
        copies[-1].start()
    for copy in copies:
        copy.wait()


def placed_rows(chunk, group, cap, index, digits, real, imag):
    pad = index.shape[1]
    span = cap + 16
    vmem = pl.BlockSpec(memory_space=pltpu.VMEM)
    return pl.pallas_call(
        functools.partial(place_kernel, chunk, cap),
        grid=(1,),
        out_shape=pltpu.HBM((group * span, 2 * FX), BF16),
        in_specs=[
            pl.BlockSpec((group, pad), lambda i: (chunk, 0), memory_space=pltpu.SMEM),
            vmem,
            vmem,
            vmem,
        ],
        out_specs=pl.BlockSpec(memory_space=pltpu.HBM),
        scratch_shapes=[pltpu.VMEM((group * span, FX), F32)] * 2
        + [pltpu.VMEM((group * span, 2 * FX), BF16), pltpu.SemaphoreType.DMA((group,))],
        compiler_params=vmem_params(16),
        cost_estimate=cost(1e6, 8e6),
        name="place",
    )(index, digits, real, imag)


def rotate(real, imag, cosine, sine):
    return real * cosine - imag * sine, real * sine + imag * cosine


def score_kernel(
    planes, inner, half_ref, turn_ref, image_ref, near_ref, far_ref, offset_ref, orient_ref, interp_ref,
    table_ref, evidence_ref,
):
    number = image_ref.shape[0]
    refs = near_ref.shape[0]
    rows_half = FY // 2
    group = 8
    off_x = offset_ref[:, 0:1]
    off_y = offset_ref[:, 1:2]
    lane = iota((number, FX), 1)

    def wave(units):
        angle = STEP * (units & (FY - 1)).astype(F32)
        return jnp.cos(angle), jnp.sin(angle)

    col_cos, col_sin = wave(-lane * off_x)
    one_cos, one_sin = wave(jnp.broadcast_to(-off_y, (number, FX)))
    ref_lane = iota((1, FX), 1)
    x1_cos, x1_sin = wave(jnp.broadcast_to(ref_lane, (refs, FX)))
    x2_cos, x2_sin = wave(jnp.broadcast_to(2 * ref_lane, (refs, FX)))

    def shifts(real, imag, c1, s1, c2, s2):
        rc, rs, ic, is_ = real * c1, real * s1, imag * c1, imag * s1
        pairs = [
            (real * c2 + imag * s2, imag * c2 - real * s2),
            (rc + is_, ic - rs),
            (real, imag),
            (rc - is_, ic + rs),
        ]
        return pairs

    def stacked(pairs):
        return jnp.concatenate(
            [jnp.concatenate([p.astype(BF16), q.astype(BF16)], axis=1) for p, q in pairs],
            axis=0,
        )

    def run(ref, first, total):
        start_cos, start_sin = wave(-(lane * off_x + first * off_y))

        def block(k, carry):
            total, cosine, sine = carry
            lefts, rights = [], []
            for i in range(group):
                r = first + k * group + i
                at = pl.multiple_of(r * 2 * FX, 2 * FX)
                at_ref = pl.multiple_of((k * group + i) * 2 * FX, 2 * FX)
                real = image_ref[:, pl.ds(at, FX)].astype(F32)
                imag = image_ref[:, pl.ds(at + FX, FX)].astype(F32)
                real, imag = rotate(real, imag, cosine, sine)
                cosine, sine = rotate(cosine, sine, one_cos, one_sin)
                lefts.append(
                    stacked(
                        shifts(
                            real, imag, turn_ref[0, r], turn_ref[1, r], turn_ref[2, r], turn_ref[3, r]
                        )
                    )
                )
                real = ref[:, pl.ds(at_ref, FX)].astype(F32)
                imag = ref[:, pl.ds(at_ref + FX, FX)].astype(F32)
                rights.append(stacked(shifts(real, imag, x1_cos, -x1_sin, x2_cos, -x2_sin)))
            total = total + lax.dot_general(
                jnp.concatenate(lefts, axis=1),
                jnp.concatenate(rights, axis=1),
                (((1,), (1,)), ((), ())),
                preferred_element_type=F32,
            )
            return total, cosine, sine

        total, _, _ = lax.fori_loop(0, rows_half // group, block, (total, start_cos, start_sin))
        return total

    half = half_ref[0]
    total = jnp.zeros((TY * number, TX * refs), F32)
    total = run(near_ref, half * rows_half, total)
    total = run(far_ref, (1 - half) * rows_half, total)
    total = total * (1.0 / math.sqrt(FY * 2 * FX))
    parts = [total[b * number : (b + 1) * number, :] for b in range(TY)]
    top = functools.reduce(jnp.maximum, parts)
    top = jnp.max(top, axis=1, keepdims=True)
    mass = sum(jnp.sum(jnp.exp(part - top), axis=1, keepdims=True) for part in parts)
    evidence = top + jnp.log(mass)
    evidence_ref[...] = jnp.broadcast_to(evidence, (number, FX))
    spot = iota((number, TX * refs), 1)
    shift_of = spot // refs
    spot = spot & (refs - 1)
    local = refs // (planes * inner)
    plane = lax.axis_index("z") - spot // (inner * local)
    plane = jnp.where(plane < 0, plane + planes, plane)
    column = lax.axis_index("x") ^ ((spot // local) & (inner - 1))
    name = (plane * inner + column) * local + (spot & (local - 1))
    slot = iota((number, FX), 1)
    table = jnp.where(slot == 32, off_x.astype(F32), 0.0)
    table = jnp.where(slot == 33, off_y.astype(F32), table)
    for l in range(LIST):
        table = jnp.where(slot == 34 + l, interp_ref[:, l : l + 1].astype(F32), table)
        for b in range(TY):
            weights = jnp.exp(parts[b] - evidence)
            for a in range(TX):
                chosen = (name == orient_ref[:, l : l + 1]) & (shift_of == a)
                value = jnp.sum(jnp.where(chosen, weights, 0.0), axis=1, keepdims=True)
                table = jnp.where(slot == l * 16 + b * TX + a, value, table)
    table_ref[...] = table


def weights_table(planes, inner, half, images, near, far, offsets, orientations, interp_index):
    number = images.shape[0]
    turn = np.arange(FY) * STEP
    turns = np.stack([np.cos(turn), np.sin(turn), np.cos(2 * turn), np.sin(2 * turn)])
    smem = pl.BlockSpec(memory_space=pltpu.SMEM)
    vmem = pl.BlockSpec(memory_space=pltpu.VMEM)
    return pl.pallas_call(
        functools.partial(score_kernel, planes, inner),
        out_shape=[jax.ShapeDtypeStruct((number, FX), F32)] * 2,
        in_specs=[smem, smem] + [vmem] * 6,
        compiler_params=vmem_params(16),
        cost_estimate=cost(3e9, 5e6),
        name="scores",
    )(
        half, jnp.asarray(turns, F32), images, near, far, offsets, orientations, interp_index
    )


def wave_table():
    shift = np.arange(NSHIFT)[:, None] - SHIFTS
    angle = STEP * ((shift * np.arange(FX)[None, :]) % FY)
    table = np.concatenate(
        [
            np.concatenate([np.cos(angle), np.sin(angle)], axis=1),
            np.concatenate([-np.sin(angle), np.cos(angle)], axis=1),
        ],
        axis=0,
    ).astype(np.float32)
    high = table.astype(jnp.bfloat16)
    low = (table - high.astype(np.float32)).astype(jnp.bfloat16)
    return np.concatenate([high, high, low], axis=0)


def gather_kernel(cap, pad, first, row_ref, table_ref, wave_ref, mats_ref, *refs):
    base_ref = refs[0] if first is None else None
    out_ref, mixed_ref, line_ref = refs[1 if first is None else 0], refs[-2], refs[-1]
    lines = out_ref.shape[0]
    members = table_ref.shape[0]
    count = mats_ref.shape[0]
    span = cap + 16
    group = row_ref.shape[0] // span
    words = pad // (2 * FX)
    low_count = count // 2
    table_high, table_low = split(table_ref[:, :64])
    picks = jnp.concatenate([table_high, table_low], axis=1)
    number = members // group
    mats = jnp.concatenate(
        [mats_ref[:low_count].reshape(low_count * FX, FX), mats_ref[low_count:].reshape(low_count * FX, FX)],
        axis=1,
    )
    def block(s, carry):
        at = pl.multiple_of(s * span, 16)
        extra = row_ref[pl.ds(at + cap, 16), :].astype(F32)
        digit = [
            jnp.concatenate(
                [extra[which * words + word : which * words + word + 1] for word in range(words)],
                axis=1,
            )[:, :cap].astype(I32)
            for which in range(4)
        ]
        r = digit[0]
        member = s * number + (digit[1] >> 1)
        front = (digit[1] & 1) == 0
        line_ref[s] = digit[2] + (digit[3] - 1) * 256
        hot = (iota((members, cap), 0) == member).astype(F32).astype(BF16)
        got = lax.dot_general(picks, hot, (((0,), (0,)), ((), ())), preferred_element_type=F32)
        got = got[:64] + got[64:]
        weight = jnp.where(front, got[0:16], got[16:32])
        off_x = got[32:33].astype(I32)
        off_y = got[33:34].astype(I32)
        interp = jnp.where(front, got[34:35], got[35:36])
        sub = iota((8, cap), 0)
        units = r * ((sub & 3) - TY // 2 - off_y) - jnp.where(sub >= 4, FY // 4, 0)
        wave = jnp.cos(STEP * (units & (FY - 1)).astype(F32))
        gate_real = sum(weight[b * TX : (b + 1) * TX] * wave[b : b + 1] for b in range(TY))
        gate_imag = sum(weight[b * TX : (b + 1) * TX] * wave[4 + b : 5 + b] for b in range(TY))
        spot = iota((NSHIFT, cap), 0) + off_x
        coef_real = jnp.zeros((NSHIFT, cap), F32)
        coef_imag = jnp.zeros((NSHIFT, cap), F32)
        for a in range(TX):
            here = spot == a - TX // 2 + SHIFTS
            coef_real = jnp.where(here, gate_real[a : a + 1], coef_real)
            coef_imag = jnp.where(here, gate_imag[a : a + 1], coef_imag)
        high, low = split(jnp.concatenate([coef_real, coef_imag], axis=0))
        coef = jnp.concatenate([high, low, high], axis=0)
        phase = lax.dot_general(
            coef, wave_ref[...], (((0,), (0,)), ((), ())), preferred_element_type=F32
        )
        values = row_ref[pl.ds(at, cap), :].astype(F32)
        real, imag = rotate(values[:, :FX], values[:, FX:], phase[:, :FX], phase[:, FX:])
        slices = jnp.concatenate([real, imag], axis=0).astype(BF16)
        column = jnp.transpose(jnp.broadcast_to(interp, (8, cap)))[:, 0:1]
        column = jnp.broadcast_to(column, (cap, FX)).astype(I32)
        column = jnp.concatenate([column, column], axis=0)
        which = jnp.where(column >= low_count, column - low_count, column)
        zero = jnp.zeros_like(slices)
        pieces = [jnp.where(which == q, slices, zero) for q in range(low_count)]
        mixed = jnp.dot(jnp.concatenate(pieces, axis=1), mats, preferred_element_type=F32)
        mixed = jnp.where(column >= low_count, mixed[:, FX:], mixed[:, :FX]).astype(BF16)
        to = pl.ds(pl.multiple_of(s * cap, 16), cap)
        mixed_ref[to, :FX] = mixed[:cap]
        mixed_ref[to, FX:] = mixed[cap:]
        return carry

    lax.fori_loop(0, group, block, 0, unroll=2)
    line = jnp.concatenate([line_ref[s] for s in range(group)], axis=1)
    tile = min(512, lines // 2)
    rows = iota((tile, group * cap), 0)
    for at in range(0, lines, tile):
        hot = jnp.where(rows == line - at, 1.0, 0.0).astype(BF16)
        value = jnp.dot(hot, mixed_ref[...], preferred_element_type=F32)
        if base_ref is not None:
            value = value + base_ref[at : at + tile, :]
        out_ref[at : at + tile, :] = value
        if first:
            piece = refs[1 + at // (lines // 2)]
            spot = at % (lines // 2)
            piece[spot : spot + tile, :] = value.astype(BF16)


def partial_lines(cap, pad, rows, table, mats, lines, first, base=None):
    group = rows.shape[0] // (cap + 16)
    shape = jax.ShapeDtypeStruct((lines, 2 * FX), F32)
    short = jax.ShapeDtypeStruct((lines // 2, 2 * FX), BF16)
    vmem = pl.BlockSpec(memory_space=pltpu.VMEM)
    extra = () if base is None else (base,)
    return pl.pallas_call(
        functools.partial(gather_kernel, cap, pad, None if extra else first),
        out_shape=(shape, short, short) if first else shape,
        in_specs=[vmem] * (4 + len(extra)),
        scratch_shapes=[
            pltpu.VMEM((group * cap, 2 * FX), BF16),
            pltpu.VMEM((group, 1, cap), I32),
        ],
        compiler_params=vmem_params(24),
        cost_estimate=cost(1e6, 1e5),
        name="lines",
    )(rows, table, jnp.asarray(wave_table()), mats, *extra)


def relay_kernel(planes, step, place_of, pieces, *refs):
    refs = list(refs)
    up_out, down_out = refs[-2:]
    downs, ups = refs[-2 - pieces : -2], refs[-2 - 2 * pieces : -2 - pieces]
    parts = refs[: -2 - 2 * pieces]
    z = lax.axis_index("z")
    lines = up_out.shape[0]
    length = lines // pieces
    tile = min(512, length)

    def send(part, came, out):
        for at in range(0, lines, tile):
            value = part[at : at + tile, :]
            if came is not None:
                spot = at % length
                value = value + came[at // length][spot : spot + tile, :].astype(F32)
            out[at : at + tile, :] = value.astype(BF16)

    for p in range(planes):
        goes_up, goes_down = p < step, p >= planes - step
        if goes_up or goes_down:

            @pl.when(z == p)
            def _(p=p, goes_up=goes_up, goes_down=goes_down):
                if goes_up:
                    part = parts[place_of[p, planes - step + p]]
                    send(part, ups if p > 0 else None, up_out)
                if goes_down:
                    part = parts[place_of[p, p - planes + step]]
                    send(part, downs if p < planes - 1 else None, down_out)


def relay(planes, step, place_of, parts, up, down):
    vmem = pl.BlockSpec(memory_space=pltpu.VMEM)
    return pl.pallas_call(
        functools.partial(relay_kernel, planes, step, place_of, len(up)),
        out_shape=[jax.ShapeDtypeStruct(parts[0].shape, BF16)] * 2,
        in_specs=[vmem] * (len(parts) + 2 * len(up)),
        compiler_params=vmem_params(14),
        cost_estimate=cost(1e6, 1e5),
        name="relay",
    )(*parts, *up, *down)


def together(*values):
    return lax.optimization_barrier(values)


def block_order(planes):
    return np.array(
        [sorted(range(planes), key=lambda d: (-abs(d - z), -d)) for z in range(planes)], np.int32
    )


def body(
    planes, inner, slab,
    images, references, offsets, orientations, interp_mats, interp_index, owners, line_index, volume_in,
):
    number = images.shape[0]
    lines = volume_in.shape[0]
    group = inner * slab
    devices = planes * group
    rows_all = number * LIST * FY
    cap = max(2, 7 * rows_all // (4 * devices))
    span = cap + 16
    pad = -(-(cap + 1) // (2 * FX)) * 2 * FX
    half = lax.axis_index("slab") % 2

    local = references.shape[0]
    width = references.shape[1]
    mine = lax.dynamic_slice_in_dim(references, half * (width // 2), width // 2, axis=1)
    block = [mine]
    for e in range(1, inner):
        block.append(lax.ppermute(mine, "x", [(i, i ^ e) for i in range(inner)]))

    place_of = np.argsort(block_order(planes), axis=1).astype(np.int32)
    index, digits, real, imag = row_slots(
        jnp.asarray(place_of),
        owners.reshape(number, LIST * FY),
        line_index,
        images,
        devices,
        group,
        pad,
    )
    block, index = together(block, index)
    block = jnp.concatenate(block, axis=0)
    near = [block]
    for shift in range(1, planes):
        near.append(lax.ppermute(block, "z", [(p, (p + shift) % planes) for p in range(planes)]))
    def place(k, index):
        return placed_rows(k, group, cap, index, digits, real, imag)

    early = min(3, planes)
    placed = [place(k, index) for k in range(early)]

    def to_members(value):
        return lax.all_to_all(
            value.reshape(group, span, 2 * FX), ("x", "slab"), 0, 0, tiled=True
        ).reshape(group * span, 2 * FX)

    got = to_members(placed[0])
    near, placed[1:3] = together(near, placed[1:3])
    near = jnp.concatenate(near, axis=0)
    far = lax.ppermute(near, "slab", [(i, i ^ 1) for i in range(slab)])
    near, far, got = together(near, far, got)
    table, evidence = weights_table(
        planes, inner, half.reshape(1).astype(I32), images, near, far, offsets, orientations,
        interp_index,
    )
    tables = lax.all_to_all(
        jnp.broadcast_to(table[None], (group,) + table.shape), ("x", "slab"), 0, 0, tiled=True
    ).reshape(group * number, FX)
    tables, placed[1] = together(tables, placed[1])
    got = [got, to_members(placed[1])]

    def lines_of(k, base=None):
        return partial_lines(cap, pad, got[k], tables, interp_mats, lines, k == 0, base)

    def fetch(k, value):
        if k < planes:
            value, placed[k] = together(value, placed[k])
            got.append(to_members(placed[k]))
        return value

    part, *short = lines_of(0)
    part, index = together(part, index)
    placed += [place(k, index) for k in range(early, planes)]
    parts = [part]
    ends = sorted({(0, 1), (planes - 1, planes - 2)})
    up = [lax.ppermute(piece, "z", ends) for piece in short]
    up[0] = fetch(2, up[0])
    down = up
    for s in range(2, planes):
        parts.append(fetch(s + 1, lines_of(s - 1)))
        up_send, down_send = relay(planes, s, place_of, parts, up, down)
        up = [lax.ppermute(up_send, "z", [(p, p + 1) for p in range(s)])]
        down = [lax.ppermute(down_send, "z", [(p, p - 1) for p in range(planes - s, planes)])]
    last = lines_of(planes - 1, volume_in)
    volume = last + jnp.concatenate(up, axis=0).astype(F32) + jnp.concatenate(down, axis=0).astype(F32)
    return volume, evidence[:, 0]


def solution(mesh):
    dom, slab = mesh.shape["dom"], mesh.shape["slab"]
    planes = dom // INNER
    fine = Mesh(mesh.devices.reshape(planes, INNER, slab), ("z", "x", "slab"))
    every = ("z", "x", "slab")
    in_specs = (
        P(every, None),
        P(("z", "x"), None),
        P(every, None),
        P(every, None),
        P(),
        P(every, None),
        P(every, None, None),
        P(every, None),
        P(every, None),
    )
    out_specs = (P(every, None), P(every))
    return jax.shard_map(
        functools.partial(body, planes, INNER, slab),
        mesh=fine,
        in_specs=in_specs,
        out_specs=out_specs,
        check_vma=False,
    )
```

time: 213 us -> 205 us (0.962)
  other arithmetic: 15.3 us -> 4.48 us
  local copies, waits for them, and re-layouts: 12.8 us -> 15.1 us
    ppermute x6 -> x10, waiting for transfers between devices: 8.2 us -> 22.7 us  [the longest x2 11.8 us: body(): up = [lax.ppermute(piece, 'z', ends) for piece in short]]
    all_to_all x6 -> x4, waiting for transfers between devices: 13.2 us -> 0.01 us  [to_members(): lax.all_to_all(value.reshape(group, span, 2 * FX), ('x', 'slab'), 0, 0, t...]
    unnamed x37 -> x46, local copies, waits for them, and re-layouts: 4.04 us -> 14.4 us
    ppermute x6 -> x10, starting transfers between devices: 18.9 us -> 28.4 us  [the longest x2 11.1 us: body(): up = [lax.ppermute(up_send, 'z', [(p, p + 1) for p in range(s)])]]
    all_to_all x6 -> x4, starting transfers between devices: 27.4 us -> 18.1 us  [to_members(): lax.all_to_all(value.reshape(group, span, 2 * FX), ('x', 'slab'), 0, 0, t...]
    convert_element_type x3 -> x0, other arithmetic: 8.56 us -> none  [body(): up = lax.ppermute(up_send.astype(BF16), 'z', [(p, p + 1) for p in range(s)])]
    add x2 -> x1, other arithmetic: 5.89 us -> 1.59 us  [body(): last + jnp.concatenate(up, axis=0).astype(F32)]
    reshape x4 -> x0, local copies, waits for them, and re-layouts: 2.92 us -> none  [the longest x1 1.48 us: body(): near = lax.all_to_all(jnp.broadcast_to(mine[None], (planes * inner,) + mi...]
  transfers between devices with their start and end apart: 13 -> 15, of which waited for: 5 -> 5; matrix products, arithmetic and copies ran while one was open for 6% -> 2% of each run, Pallas kernels for 48% -> 45%
where the time goes in v2:
time: 205 us; the launch traced here: 204 us
  Pallas kernels  102 us (50%)
  starting transfers between devices  47 us (23%)
  waiting for transfers between devices  25.1 us (12%)
  local copies, waits for them, and re-layouts  15.1 us (7%)
  blocking collectives  9.01 us (4%)
  other arithmetic  4.48 us (2%)
    pallas_call x4, Pallas kernels, partial_lines(): pl.pallas_call(functools.partial(gather_kernel, cap, pad, None if extra e...  49.7 us
    pallas_call x4, Pallas kernels, placed_rows(): pl.pallas_call(functools.partial(place_kernel, chunk, cap), grid=(1,), ou...  33.4 us
    all_to_all x4, starting transfers between devices, to_members(): lax.all_to_all(value.reshape(group, span, 2 * FX), ('x', 'slab'), 0, 0, t...  18.1 us
    unnamed x46, local copies, waits for them, and re-layouts  14.4 us
    ppermute x2, waiting for transfers between devices, body(): up = [lax.ppermute(piece, 'z', ends) for piece in short]  11.8 us
    ppermute x2, starting transfers between devices, body(): up = [lax.ppermute(up_send, 'z', [(p, p + 1) for p in range(s)])]  11.1 us
    pallas_call x1, Pallas kernels, weights_table(): pl.pallas_call(functools.partial(score_kernel, planes, inner), out_shape=...  10.2 us
    all_to_all x1, blocking collectives, body(): lax.all_to_all(jnp.broadcast_to(table[None], (group,) + table.shape), ('x...  9.01 us
  transfers between devices with their start and end apart: 15, of which 5 were waited for; matrix products, arithmetic and copies ran while one was open for 2% of the time, Pallas kernels for 45%

profile of v2, /device:TPU:0, one launch (start us, length us, event | category | flops | bytes accessed | tf_op | source)
XLA Modules:
  0.0 204.0 jit_solution(7968513246833232555)
XLA Ops:
  1.7 3.0 %collective-permute-start = (bf16[2,32768]{1,0:T(2,128)(2,1)S(1)}, bf16[2,32768]{1,0:T(2,128)(2,1)S(1)}, u32[]{:S(2)}, u32[]{:S(2)}) collective-permute-start(bf16[2,32768]{1,0:T(2,128)(2,1)S(1)} %constant_dynamic-slice_fusion), channel_id=1, source_target_pairs={{0,4},{4,0},{1,5},{5,1},{2,6},{6,2},{3,7},{7,3},{8,12},{12,8},{9,1... | collective-permute-start | bytes 393224 | tf_op jit(solution)/shard_map/ppermute | solution.py:513
  5.4 1.6 copy-done.12
  8.5 4.4 %slots.1 = (s32[32,512]{1,0:T(8,128)S(1)}, f32[128,512]{1,0:T(8,128)S(1)}, f32[4096,128]{1,0:T(8,128)S(1)}, f32[4096,128]{1,0:T(8,128)S(1)}) custom-call(s32[4,4]{1,0:T(4,128)S(1)} %copy-done.17, s32[16,512]{1,0:T(8,128)S(1)} %bitcast.17, s32[16,512]{1,0:T(8,128)S(1)} %copy-done.15, bf16[16,65536]{1,0:T(8,128)(2,1)S(1)} %copy-done.12), custom_call_target="tpu_custom_call" | custom-call | flops 3000000000 | bytes 12000000 | tf_op jit(solution)/shard_map/slots/pallas_call | solution.py:110
  13.2 1.6 collective-permute-start.1
  14.8 2.6 %collective-permute-start.2 = (bf16[4,32768]{1,0:T(4,128)(2,1)S(1)}, bf16[4,32768]{1,0:T(4,128)(2,1)S(1)}, u32[]{:S(2)}, u32[]{:S(2)}) collective-permute-start(bf16[4,32768]{1,0:T(4,128)(2,1)S(1)} %pad_maximum_fusion.1), channel_id=1, source_target_pairs={{0,16},{8,24},{16,0},{24,8},{1,17},{9,25},{17,1},{25,9},{2,18},{10... | collective-permute-start | bytes 786440 | tf_op jit(solution)/shard_map/ppermute | solution.py:529
  18.8 8.1 %place.6 = bf16[3712,256]{1,0:T(8,128)(2,1)} custom-call(s32[32,512]{1,0:T(8,128)S(1)} %get-tuple-element.54.index_ref, f32[128,512]{1,0:T(8,128)S(1)} %get-tuple-element.39.digit_ref, f32[4096,128]{1,0:T(8,128)S(1)} %get-tuple-element.40.real_ref, f32[4096,128]{1,0:T(8,128)S(1)} %get-tuple-element.41.imag_ref), custom_call_target="tpu_custom_call" | custom-call | flops 1000000 | bytes 8000000 | tf_op jit(solution)/shard_map/place/pallas_call | solution.py:171
  26.9 4.3 %all-to-all-start = ((bf16[8,464,256]{2,1,0:T(8,128)(2,1)}), bf16[8,464,256]{2,1,0:T(8,128)(2,1)}, u32[]{:S(2)}, u32[]{:S(2)}) async-start(bf16[8,464,256]{2,1,0:T(8,128)(2,1)} %bitcast.21), calls=%async_computation | async-start | bytes 3801088 | tf_op jit(solution)/shard_map/all_to_all | solution.py:537
  32.9 9.1 %place.5 = bf16[3712,256]{1,0:T(8,128)(2,1)} custom-call(s32[32,512]{1,0:T(8,128)S(1)} %get-tuple-element.54.index_ref, f32[128,512]{1,0:T(8,128)S(1)} %get-tuple-element.39.digit_ref, f32[4096,128]{1,0:T(8,128)S(1)} %get-tuple-element.40.real_ref, f32[4096,128]{1,0:T(8,128)S(1)} %copy-done.2), custom_call_target="tpu_custom_call" | custom-call | flops 1000000 | bytes 8000000 | tf_op jit(solution)/shard_map/place/pallas_call | solution.py:171
  42.0 8.2 %place.4 = bf16[3712,256]{1,0:T(8,128)(2,1)} custom-call(s32[32,512]{1,0:T(8,128)S(1)} %get-tuple-element.54.index_ref, f32[128,512]{1,0:T(8,128)S(1)} %get-tuple-element.39.digit_ref, f32[4096,128]{1,0:T(8,128)S(1)} %get-tuple-element.40.real_ref, f32[4096,128]{1,0:T(8,128)S(1)} %copy-done.2), custom_call_target="tpu_custom_call" | custom-call | flops 1000000 | bytes 8000000 | tf_op jit(solution)/shard_map/place/pallas_call | solution.py:171
  50.3 2.6 %pad_maximum_fusion.near_ref = bf16[16,32768]{1,0:T(8,128)(2,1)} fusion(bf16[4,32768]{1,0:T(4,128)(2,1)} %collective-permute-done.3, bf16[4,32768]{1,0:T(4,128)(2,1)S(1)} %collective-permute-done.2, bf16[4,32768]{1,0:T(4,128)(2,1)S(1)} %collective-permute-done.1, bf16[4,32768]{1,0:T(4,128)(2,1)S(1)} %pad_maximum_fusion.1), kind=kLoop, calls=%fused_computation.1 | loop fusion | flops 4194304 | bytes 2097152 | tf_op jit(solution)/shard_map/concatenate | solution.py:543
  53.7 2.4 %collective-permute-done.4.far_ref = bf16[16,32768]{1,0:T(8,128)(2,1)} collective-permute-done((bf16[16,32768]{1,0:T(8,128)(2,1)}, bf16[16,32768]{1,0:T(8,128)(2,1)}, u32[]{:S(2)}, u32[]{:S(2)}) %collective-permute-start.4) | collective-permute-done | bytes 1048608 | tf_op jit(solution)/shard_map/ppermute | solution.py:544
  56.1 1.6 copy-done.13
  57.7 10.2 %scores.1 = (f32[16,128]{1,0:T(8,128)S(1)}, f32[16,128]{1,0:T(8,128)S(1)}) custom-call(s32[1]{0:T(128)} %bitcast.half_ref, f32[4,256]{1,0:T(4,128)S(1)} %copy-done.16, bf16[16,65536]{1,0:T(8,128)(2,1)S(1)} %copy-done.13, bf16[16,32768]{1,0:T(8,128)(2,1)} %pad_maximum_fusion.near_ref, bf16[16,32768]{1,0:T(8,128)(2,1)} %collective-permute-done.4.far_ref, ...), custom_call_target="tpu_custom_call" | custom-call | flops 3000000000 | bytes 5000000 | tf_op jit(solution)/shard_map/scores/pallas_call | solution.py:306
  68.0 9.0 %all_to_all.25 = f32[8,16,128]{2,1,0:T(8,128)S(1)} all-to-all(f32[8,16,128]{2,1,0:T(8,128)S(1)} %broadcast_in_dim.2), channel_id=1, replica_groups=mesh['z'=4,'x'=2,'slab'=4] {'x','slab'}, dimensions={0} | all-to-all | bytes 131072 | tf_op jit(solution)/shard_map/all_to_all | solution.py:550
  77.0 4.5 %all-to-all-start.2 = ((bf16[8,464,256]{2,1,0:T(8,128)(2,1)}), bf16[8,464,256]{2,1,0:T(8,128)(2,1)}, u32[]{:S(2)}, u32[]{:S(2)}) async-start(bf16[8,464,256]{2,1,0:T(8,128)(2,1)} %bitcast.20), calls=%async_computation.2 | async-start | bytes 3801088 | tf_op jit(solution)/shard_map/all_to_all | solution.py:537
  81.6 12.4 %lines.5 = (f32[2048,256]{1,0:T(8,128)S(1)}, bf16[1024,256]{1,0:T(8,128)(2,1)S(1)}, bf16[1024,256]{1,0:T(8,128)(2,1)S(1)}) custom-call(bf16[3712,256]{1,0:T(8,128)(2,1)} %bitcast.2.row_ref, f32[128,128]{1,0:T(8,128)S(1)} %bitcast.13, bf16[144,256]{1,0:T(8,128)(2,1)S(1)} %copy-done.9, bf16[8,128,128]{2,1,0:T(8,128)(2,1)S(1)} %copy-done.7), custom_call_target="tpu_custom_call" | custom-call | flops 1000000 | bytes 100000 | tf_op jit(solution)/shard_map/lines/pallas_call | solution.py:426
  97.4 11.8 %collective-permute-done.5.refs_2_.refs_4_ = bf16[1024,256]{1,0:T(8,128)(2,1)S(1)} collective-permute-done((bf16[1024,256]{1,0:T(8,128)(2,1)S(1)}, bf16[1024,256]{1,0:T(8,128)(2,1)S(1)}, u32[]{:S(2)}, u32[]{:S(2)}) %collective-permute-start.5) | collective-permute-done | bytes 524320 | tf_op jit(solution)/shard_map/ppermute | solution.py:570
  109.2 4.3 %all-to-all-start.4 = ((bf16[8,464,256]{2,1,0:T(8,128)(2,1)}), bf16[8,464,256]{2,1,0:T(8,128)(2,1)}, u32[]{:S(2)}, u32[]{:S(2)}) async-start(bf16[8,464,256]{2,1,0:T(8,128)(2,1)} %bitcast.18), calls=%async_computation.4 | async-start | bytes 3801088 | tf_op jit(solution)/shard_map/all_to_all | solution.py:537
  113.5 4.4 %collective-permute-start.6 = (bf16[1024,256]{1,0:T(8,128)(2,1)}, bf16[1024,256]{1,0:T(8,128)(2,1)S(1)}, u32[]{:S(2)}, u32[]{:S(2)}) collective-permute-start(bf16[1024,256]{1,0:T(8,128)(2,1)} %copy-done.14), channel_id=1, source_target_pairs={{0,8},{24,16},{1,9},{25,17},{2,10},{26,18},{3,11},{27,19},{4,12},{... | collective-permute-start | bytes 1572872 | tf_op jit(solution)/shard_map/ppermute | solution.py:570
  120.4 8.0 %place.7 = bf16[3712,256]{1,0:T(8,128)(2,1)} custom-call(s32[32,512]{1,0:T(8,128)S(1)} %copy-done.11, f32[128,512]{1,0:T(8,128)S(1)} %get-tuple-element.39.digit_ref, f32[4096,128]{1,0:T(8,128)S(1)} %get-tuple-element.40.real_ref, f32[4096,128]{1,0:T(8,128)S(1)} %copy-done.3), custom_call_target="tpu_custom_call" | custom-call | flops 1000000 | bytes 8000000 | tf_op jit(solution)/shard_map/place/pallas_call | solution.py:171
  128.4 12.5 %lines.4.refs_1_ = f32[2048,256]{1,0:T(8,128)S(1)} custom-call(bf16[3712,256]{1,0:T(8,128)(2,1)} %bitcast.5.row_ref, f32[128,128]{1,0:T(8,128)S(1)} %bitcast.14, bf16[144,256]{1,0:T(8,128)(2,1)S(1)} %copy-done.9, bf16[8,128,128]{2,1,0:T(8,128)(2,1)S(1)} %copy-done.7), custom_call_target="tpu_custom_call" | custom-call | flops 1000000 | bytes 100000 | tf_op jit(solution)/shard_map/lines/pallas_call | solution.py:426
  142.4 3.0 %collective-permute-start.7 = (bf16[2048,256]{1,0:T(8,128)(2,1)}, bf16[2048,256]{1,0:T(8,128)(2,1)}, u32[]{:S(2)}, u32[]{:S(2)}) collective-permute-start(bf16[2048,256]{1,0:T(8,128)(2,1)} %get-tuple-element.63), channel_id=1, source_target_pairs={{0,8},{8,16},{1,9},{9,17},{2,10},{10,18},{3,11},{11,19},{4,12},{12... | collective-permute-start | bytes 3145736 | tf_op jit(solution)/shard_map/ppermute | solution.py:576
  145.4 1.7 collective-permute-start.8
  147.1 4.9 %all-to-all-start.3 = ((bf16[8,464,256]{2,1,0:T(8,128)(2,1)}), bf16[8,464,256]{2,1,0:T(8,128)(2,1)}, u32[]{:S(2)}, u32[]{:S(2)}) async-start(bf16[8,464,256]{2,1,0:T(8,128)(2,1)} %bitcast.19), calls=%async_computation.3 | async-start | bytes 3801088 | tf_op jit(solution)/shard_map/all_to_all | solution.py:537
  152.0 12.5 %lines.7.refs_2_ = f32[2048,256]{1,0:T(8,128)S(1)} custom-call(bf16[3712,256]{1,0:T(8,128)(2,1)} %bitcast.9.row_ref, f32[128,128]{1,0:T(8,128)S(1)} %bitcast.15, bf16[144,256]{1,0:T(8,128)(2,1)S(1)} %copy-done.9, bf16[8,128,128]{2,1,0:T(8,128)(2,1)S(1)} %copy-done.7), custom_call_target="tpu_custom_call" | custom-call | flops 1000000 | bytes 100000 | tf_op jit(solution)/shard_map/lines/pallas_call | solution.py:426
  164.5 3.5 %collective-permute-done.7.refs_3_ = bf16[2048,256]{1,0:T(8,128)(2,1)} collective-permute-done((bf16[2048,256]{1,0:T(8,128)(2,1)}, bf16[2048,256]{1,0:T(8,128)(2,1)}, u32[]{:S(2)}, u32[]{:S(2)}) %collective-permute-start.7) | collective-permute-done | bytes 1048608 | tf_op jit(solution)/shard_map/ppermute | solution.py:576
  168.0 3.0 %relay.3 = (bf16[2048,256]{1,0:T(8,128)(2,1)}, bf16[2048,256]{1,0:T(8,128)(2,1)}) custom-call(f32[2048,256]{1,0:T(8,128)S(1)} %copy-done.6, f32[2048,256]{1,0:T(8,128)S(1)} %lines.4.refs_1_, f32[2048,256]{1,0:T(8,128)S(1)} %lines.7.refs_2_, bf16[2048,256]{1,0:T(8,128)(2,1)} %collective-permute-done.7.refs_3_, bf16[2048,256]{1,0:T(8,128)(2,1)} %collective-permute-done.8.refs_4_), custom_call_target="tpu_custom_call" | custom-call | flops 1000000 | bytes 100000 | tf_op jit(solution)/shard_map/relay/pallas_call | solution.py:474
  172.3 8.1 %collective-permute-start.9 = (bf16[2048,256]{1,0:T(8,128)(2,1)}, bf16[2048,256]{1,0:T(8,128)(2,1)S(1)}, u32[]{:S(2)}, u32[]{:S(2)}) collective-permute-start(bf16[2048,256]{1,0:T(8,128)(2,1)} %get-tuple-element.65), channel_id=1, source_target_pairs={{0,8},{8,16},{16,24},{1,9},{9,17},{17,25},{2,10},{10,18},{18,26},{... | collective-permute-start | bytes 3145736 | tf_op jit(solution)/shard_map/ppermute | solution.py:576
  181.0 1.6 copy-done.8
  182.6 12.4 %lines.6 = f32[2048,256]{1,0:T(8,128)S(1)} custom-call(bf16[3712,256]{1,0:T(8,128)(2,1)} %bitcast.7.row_ref, f32[128,128]{1,0:T(8,128)S(1)} %bitcast.16, bf16[144,256]{1,0:T(8,128)(2,1)S(1)} %copy-done.9, bf16[8,128,128]{2,1,0:T(8,128)(2,1)S(1)} %copy-done.7, f32[2048,256]{1,0:T(8,128)S(1)} %copy-done.8), custom_call_target="tpu_custom_call" | custom-call | flops 1000000 | bytes 100000 | tf_op jit(solution)/shard_map/lines/pallas_call | solution.py:426
  195.0 6.1 %collective-permute-done.10 = bf16[2048,256]{1,0:T(8,128)(2,1)S(1)} collective-permute-done((bf16[2048,256]{1,0:T(8,128)(2,1)}, bf16[2048,256]{1,0:T(8,128)(2,1)S(1)}, u32[]{:S(2)}, u32[]{:S(2)}) %collective-permute-start.10) | collective-permute-done | bytes 1048608 | tf_op jit(solution)/shard_map/ppermute | solution.py:577
  202.4 1.6 convert_add_fusion
  (63 shorter events, 17.9 us)
Async XLA Ops:
  0.6 1.0 copy-start
  1.7 11.2 %collective-permute-start = (bf16[2,32768]{1,0:T(2,128)(2,1)S(1)}, bf16[2,32768]{1,0:T(2,128)(2,1)S(1)}, u32[]{:S(2)}, u32[]{:S(2)}) collective-permute-start(bf16[2,32768]{1,0:T(2,128)(2,1)S(1)} %constant_dynamic-slice_fusion), channel_id=1, source_target_pairs={{0,4},{4,0},{1,5},{5,1},{2,6},{6,2},{3,7},{7,3},{8,12},{12,8},{9,1... | collective-permute-start | bytes 393224 | tf_op jit(solution)/shard_map/ppermute | solution.py:513
  5.4 1.6 copy-start.12
  12.9 14.0 %copy-start.1 = (f32[4096,128]{1,0:T(8,128)}, f32[4096,128]{1,0:T(8,128)S(1)}, u32[]{:S(2)}) copy-start(f32[4096,128]{1,0:T(8,128)S(1)} %get-tuple-element.41.imag_ref) | copy-start | bytes 6291460
  12.9 29.1 %copy-start.10 = (s32[32,512]{1,0:T(8,128)}, s32[32,512]{1,0:T(8,128)S(1)}, u32[]{:S(2)}) copy-start(s32[32,512]{1,0:T(8,128)S(1)} %get-tuple-element.54.index_ref) | copy-start | bytes 196612
  13.2 37.1 %collective-permute-start.1 = (bf16[4,32768]{1,0:T(4,128)(2,1)S(1)}, bf16[4,32768]{1,0:T(4,128)(2,1)S(1)}, u32[]{:S(2)}, u32[]{:S(2)}) collective-permute-start(bf16[4,32768]{1,0:T(4,128)(2,1)S(1)} %pad_maximum_fusion.1), channel_id=1, source_target_pairs={{0,8},{8,16},{16,24},{24,0},{1,9},{9,17},{17,25},{25,1},{2,10},{10... | collective-permute-start | bytes 786440 | tf_op jit(solution)/shard_map/ppermute | solution.py:529
  14.8 35.5 %collective-permute-start.2 = (bf16[4,32768]{1,0:T(4,128)(2,1)S(1)}, bf16[4,32768]{1,0:T(4,128)(2,1)S(1)}, u32[]{:S(2)}, u32[]{:S(2)}) collective-permute-start(bf16[4,32768]{1,0:T(4,128)(2,1)S(1)} %pad_maximum_fusion.1), channel_id=1, source_target_pairs={{0,16},{8,24},{16,0},{24,8},{1,17},{9,25},{17,1},{25,9},{2,18},{10... | collective-permute-start | bytes 786440 | tf_op jit(solution)/shard_map/ppermute | solution.py:529
  17.4 32.9 %collective-permute-start.3 = (bf16[4,32768]{1,0:T(4,128)(2,1)S(1)}, bf16[4,32768]{1,0:T(4,128)(2,1)}, u32[]{:S(2)}, u32[]{:S(2)}) collective-permute-start(bf16[4,32768]{1,0:T(4,128)(2,1)S(1)} %pad_maximum_fusion.1), channel_id=1, source_target_pairs={{0,24},{8,0},{16,8},{24,16},{1,25},{9,1},{17,9},{25,17},{2,26},{10... | collective-permute-start | bytes 786440 | tf_op jit(solution)/shard_map/ppermute | solution.py:529
  26.9 29.2 %all-to-all-start = ((bf16[8,464,256]{2,1,0:T(8,128)(2,1)}), bf16[8,464,256]{2,1,0:T(8,128)(2,1)}, u32[]{:S(2)}, u32[]{:S(2)}) async-start(bf16[8,464,256]{2,1,0:T(8,128)(2,1)} %bitcast.21), calls=%async_computation | async-start | bytes 3801088 | tf_op jit(solution)/shard_map/all_to_all | solution.py:537
  31.3 1.6 copy-start.2
  50.2 3.3 %copy-start.18 = (s32[16,2]{0,1:T(2,128)S(1)}, s32[16,2]{0,1:T(2,128)}, u32[]{:S(2)}) copy-start(s32[16,2]{0,1:T(2,128)} %param.17) | copy-start | bytes 388
  50.2 3.3 %copy-start.19 = (s32[16,2]{0,1:T(2,128)S(1)}, s32[16,2]{0,1:T(2,128)}, u32[]{:S(2)}) copy-start(s32[16,2]{0,1:T(2,128)} %param.18) | copy-start | bytes 388
  50.3 3.4 %copy-start.20 = (s32[16,2]{0,1:T(2,128)S(1)}, s32[16,2]{0,1:T(2,128)}, u32[]{:S(2)}) copy-start(s32[16,2]{0,1:T(2,128)} %param.20) | copy-start | bytes 388
  50.3 5.8 %copy-start.16 = (f32[4,256]{1,0:T(4,128)S(1)}, f32[4,256]{1,0:T(4,128)}, u32[]{:S(2)}) copy-start(f32[4,256]{1,0:T(4,128)} %constant.29.clone.turn_ref) | copy-start | bytes 12292
  52.9 3.2 %collective-permute-start.4 = (bf16[16,32768]{1,0:T(8,128)(2,1)}, bf16[16,32768]{1,0:T(8,128)(2,1)}, u32[]{:S(2)}, u32[]{:S(2)}) collective-permute-start(bf16[16,32768]{1,0:T(8,128)(2,1)} %pad_maximum_fusion.near_ref), channel_id=1, source_target_pairs={{0,1},{1,0},{2,3},{3,2},{4,5},{5,4},{6,7},{7,6},{8,9},{9,8},{10,11... | collective-permute-start | bytes 3145736 | tf_op jit(solution)/shard_map/ppermute | solution.py:544
  56.1 1.6 copy-start.13
  68.0 13.6 %copy-start.7 = (bf16[8,128,128]{2,1,0:T(8,128)(2,1)S(1)}, bf16[8,128,128]{2,1,0:T(8,128)(2,1)}, u32[]{:S(2)}) copy-start(bf16[8,128,128]{2,1,0:T(8,128)(2,1)} %mats_ref.7) | copy-start | bytes 786436
  68.0 13.6 %copy-start.9 = (bf16[144,256]{1,0:T(8,128)(2,1)S(1)}, bf16[144,256]{1,0:T(8,128)(2,1)}, u32[]{:S(2)}) copy-start(bf16[144,256]{1,0:T(8,128)(2,1)} %constant.30.clone.wave_ref) | copy-start | bytes 221188
  77.0 32.2 %all-to-all-start.2 = ((bf16[8,464,256]{2,1,0:T(8,128)(2,1)}), bf16[8,464,256]{2,1,0:T(8,128)(2,1)}, u32[]{:S(2)}, u32[]{:S(2)}) async-start(bf16[8,464,256]{2,1,0:T(8,128)(2,1)} %bitcast.20), calls=%async_computation.2 | async-start | bytes 3801088 | tf_op jit(solution)/shard_map/all_to_all | solution.py:537
  93.9 1.3 copy-start.4
  96.1 13.1 %collective-permute-start.5 = (bf16[1024,256]{1,0:T(8,128)(2,1)S(1)}, bf16[1024,256]{1,0:T(8,128)(2,1)S(1)}, u32[]{:S(2)}, u32[]{:S(2)}) collective-permute-start(bf16[1024,256]{1,0:T(8,128)(2,1)S(1)} %get-tuple-element.58), channel_id=1, source_target_pairs={{0,8},{24,16},{1,9},{25,17},{2,10},{26,18},{3,11},{27,19},{4,12},{... | collective-permute-start | bytes 1572872 | tf_op jit(solution)/shard_map/ppermute | solution.py:570
  109.2 37.9 %all-to-all-start.4 = ((bf16[8,464,256]{2,1,0:T(8,128)(2,1)}), bf16[8,464,256]{2,1,0:T(8,128)(2,1)}, u32[]{:S(2)}, u32[]{:S(2)}) async-start(bf16[8,464,256]{2,1,0:T(8,128)(2,1)} %bitcast.18), calls=%async_computation.4 | async-start | bytes 3801088 | tf_op jit(solution)/shard_map/all_to_all | solution.py:537
  113.5 27.4 %collective-permute-start.6 = (bf16[1024,256]{1,0:T(8,128)(2,1)}, bf16[1024,256]{1,0:T(8,128)(2,1)S(1)}, u32[]{:S(2)}, u32[]{:S(2)}) collective-permute-start(bf16[1024,256]{1,0:T(8,128)(2,1)} %copy-done.14), channel_id=1, source_target_pairs={{0,8},{24,16},{1,9},{25,17},{2,10},{26,18},{3,11},{27,19},{4,12},{... | collective-permute-start | bytes 1572872 | tf_op jit(solution)/shard_map/ppermute | solution.py:570
  118.0 1.6 copy-start.3
  128.4 12.5 %copy-start.5 = (f32[2048,256]{1,0:T(8,128)S(1)}, f32[2048,256]{1,0:T(8,128)}, u32[]{:S(2)}) copy-start(f32[2048,256]{1,0:T(8,128)} %copy-done.4) | copy-start | bytes 6291460
  142.4 25.6 %collective-permute-start.7 = (bf16[2048,256]{1,0:T(8,128)(2,1)}, bf16[2048,256]{1,0:T(8,128)(2,1)}, u32[]{:S(2)}, u32[]{:S(2)}) collective-permute-start(bf16[2048,256]{1,0:T(8,128)(2,1)} %get-tuple-element.63), channel_id=1, source_target_pairs={{0,8},{8,16},{1,9},{9,17},{2,10},{10,18},{3,11},{11,19},{4,12},{12... | collective-permute-start | bytes 3145736 | tf_op jit(solution)/shard_map/ppermute | solution.py:576
  145.4 22.6 %collective-permute-start.8 = (bf16[2048,256]{1,0:T(8,128)(2,1)}, bf16[2048,256]{1,0:T(8,128)(2,1)}, u32[]{:S(2)}, u32[]{:S(2)}) collective-permute-start(bf16[2048,256]{1,0:T(8,128)(2,1)} %get-tuple-element.64), channel_id=1, source_target_pairs={{16,8},{24,16},{17,9},{25,17},{18,10},{26,18},{19,11},{27,19},{20,... | collective-permute-start | bytes 3145736 | tf_op jit(solution)/shard_map/ppermute | solution.py:577
  147.1 33.9 %all-to-all-start.3 = ((bf16[8,464,256]{2,1,0:T(8,128)(2,1)}), bf16[8,464,256]{2,1,0:T(8,128)(2,1)}, u32[]{:S(2)}, u32[]{:S(2)}) async-start(bf16[8,464,256]{2,1,0:T(8,128)(2,1)} %bitcast.19), calls=%async_computation.3 | async-start | bytes 3801088 | tf_op jit(solution)/shard_map/all_to_all | solution.py:537
  152.0 16.0 %copy-start.6 = (f32[2048,256]{1,0:T(8,128)S(1)}, f32[2048,256]{1,0:T(8,128)}, u32[]{:S(2)}) copy-start(f32[2048,256]{1,0:T(8,128)} %copy-done.4) | copy-start | bytes 6291460
  171.0 30.1 %collective-permute-start.10 = (bf16[2048,256]{1,0:T(8,128)(2,1)}, bf16[2048,256]{1,0:T(8,128)(2,1)S(1)}, u32[]{:S(2)}, u32[]{:S(2)}) collective-permute-start(bf16[2048,256]{1,0:T(8,128)(2,1)} %get-tuple-element.66), channel_id=1, source_target_pairs={{8,0},{16,8},{24,16},{9,1},{17,9},{25,17},{10,2},{18,10},{26,18},{... | collective-permute-start | bytes 3145736 | tf_op jit(solution)/shard_map/ppermute | solution.py:577
  172.3 30.1 %collective-permute-start.9 = (bf16[2048,256]{1,0:T(8,128)(2,1)}, bf16[2048,256]{1,0:T(8,128)(2,1)S(1)}, u32[]{:S(2)}, u32[]{:S(2)}) collective-permute-start(bf16[2048,256]{1,0:T(8,128)(2,1)} %get-tuple-element.65), channel_id=1, source_target_pairs={{0,8},{8,16},{16,24},{1,9},{9,17},{17,25},{2,10},{10,18},{18,26},{... | collective-permute-start | bytes 3145736 | tf_op jit(solution)/shard_map/ppermute | solution.py:576
  181.0 1.6 copy-start.8
  (4 other events, 3.1 us)

commit v3 on v2

--- a/solution.py
+++ b/solution.py
@@ -41,19 +41,27 @@
     return lax.broadcasted_iota(I32, shape, axis)
 
 
+def in_hbm(value):
+    return pltpu.with_memory_space_constraint(value, pltpu.HBM)
+
+
 def split(value):
     high = value.astype(BF16)
     return high, (value - high.astype(F32)).astype(BF16)
 
 
 def slot_kernel(
-    dests, group, pad, place_ref, owner_ref, line_ref, image_ref,
-    index_ref, digit_ref, real_ref, imag_ref, hot_ref,
+    dests, group, pad, place_of, owner_ref, line_from, image_from,
+    index_ref, digit_ref, real_ref, imag_ref, hot_ref, line_ref, image_ref, sems,
 ):
     number = owner_ref.shape[0]
     blocks = number * LIST
     planes = dests // group
     z = lax.axis_index("z")
+    lines_in = pltpu.make_async_copy(line_from, line_ref, sems.at[0])
+    lines_in.start()
+    images_in = pltpu.make_async_copy(image_from, image_ref, sems.at[1])
+    images_in.start()
 
     def widen(k, carry):
         for i in range(8):
@@ -64,12 +72,14 @@
             imag_ref[to, :] = image_ref[:, pl.ds(at + FX, FX)].astype(F32)
         return carry
 
-    lax.fori_loop(0, FY // 8, widen, 0)
     owner = owner_ref[...]
     plane = owner // group
     chunk = jnp.zeros_like(owner)
     for k in range(planes):
-        chunk = jnp.where(plane == k, place_ref[z, k], chunk)
+        at = functools.reduce(
+            lambda value, p: jnp.where(z == p, int(place_of[p, k]), value), range(planes), 0
+        )
+        chunk = jnp.where(plane == k, at, chunk)
     dest = chunk * group + (owner & (group - 1))
     owner_rows = iota((dests, FY), 0)
     for b in range(blocks):
@@ -78,6 +88,7 @@
         hot_ref[b * dests : (b + 1) * dests, :] = hot.astype(F32).astype(BF16)
     before = (iota((FY, FY), 0) < iota((FY, FY), 1)).astype(F32).astype(BF16)
     prefix = jnp.dot(hot_ref[...], before, preferred_element_type=F32)
+    lines_in.wait()
     running = jnp.zeros((dests, 1), F32)
     lane = iota((1, FY), 1).astype(F32)
     ranks = iota((pad, FY), 0)
@@ -103,29 +114,37 @@
     digit_ref[...] = total
     row = total[:dests].astype(I32) * number + (total[dests : 2 * dests].astype(I32) >> 1)
     index_ref[...] = jnp.where(iota((dests, pad), 1) == pad - 1, running.astype(I32), row)
-
-
-def row_slots(places, owners, lines, images, dests, group, pad):
+    images_in.wait()
+    lax.fori_loop(0, FY // 8, widen, 0)
+
+
+def row_slots(place_of, owners, lines, images, dests, group, pad):
     number, width = images.shape
     return pl.pallas_call(
-        functools.partial(slot_kernel, dests, group, pad),
+        functools.partial(slot_kernel, dests, group, pad, place_of),
         out_shape=(
             jax.ShapeDtypeStruct((dests, pad), I32),
             jax.ShapeDtypeStruct((4 * dests, pad), F32),
             pltpu.VMEM((number * FY, FX), F32),
             pltpu.VMEM((number * FY, FX), F32),
         ),
-        in_specs=[pl.BlockSpec(memory_space=pltpu.SMEM)]
-        + [pl.BlockSpec(memory_space=pltpu.VMEM)] * 3,
-        scratch_shapes=[pltpu.VMEM((number * LIST * dests, FY), BF16)],
-        compiler_params=vmem_params(24),
+        in_specs=[pl.BlockSpec(memory_space=pltpu.VMEM)]
+        + [pl.BlockSpec(memory_space=pltpu.HBM)] * 2,
+        scratch_shapes=[
+            pltpu.VMEM((number * LIST * dests, FY), BF16),
+            pltpu.VMEM(lines.shape, I32),
+            pltpu.VMEM(images.shape, BF16),
+            pltpu.SemaphoreType.DMA((2,)),
+        ],
+        compiler_params=vmem_params(20),
         cost_estimate=cost(3e9, 12e6),
         name="slots",
-    )(places, owners, lines, images)
+    )(owners, in_hbm(lines), in_hbm(images))
 
 
 def place_kernel(
-    chunk, cap, index_ref, digit_ref, real_ref, imag_ref, out_ref, left_ref, right_ref, held, sems
+    chunk, cap, index_ref, digit_ref, real_ref, imag_ref, out_ref, token_ref, left_ref, right_ref,
+    held, sems,
 ):
     group, pad = index_ref.shape
     dests = digit_ref.shape[0] // 4
@@ -135,6 +154,7 @@
 
     left_ref[...] = zeros
     right_ref[...] = zeros
+    token_ref[...] = jnp.zeros_like(token_ref)
     copies = []
     for d in range(group):
         start = d * span
@@ -171,18 +191,18 @@
     return pl.pallas_call(
         functools.partial(place_kernel, chunk, cap),
         grid=(1,),
-        out_shape=pltpu.HBM((group * span, 2 * FX), BF16),
+        out_shape=(pltpu.HBM((group * span, 2 * FX), BF16), jax.ShapeDtypeStruct((8, FX), F32)),
         in_specs=[
             pl.BlockSpec((group, pad), lambda i: (chunk, 0), memory_space=pltpu.SMEM),
             vmem,
             vmem,
             vmem,
         ],
-        out_specs=pl.BlockSpec(memory_space=pltpu.HBM),
+        out_specs=(pl.BlockSpec(memory_space=pltpu.HBM), vmem),
         scratch_shapes=[pltpu.VMEM((group * span, FX), F32)] * 2
         + [pltpu.VMEM((group * span, 2 * FX), BF16), pltpu.SemaphoreType.DMA((group,))],
-        compiler_params=vmem_params(16),
-        cost_estimate=cost(1e6, 8e6),
+        compiler_params=vmem_params(12),
+        cost_estimate=cost(1e5, 1e5),
         name="place",
     )(index, digits, real, imag)
 
@@ -192,13 +212,23 @@
 
 
 def score_kernel(
-    planes, inner, half_ref, turn_ref, image_ref, near_ref, far_ref, offset_ref, orient_ref, interp_ref,
-    table_ref, evidence_ref,
+    planes, inner, half_ref, turn_ref, image_from, near_ref, far_ref, offset_ref, orient_ref,
+    interp_ref, token_ref, table_ref, evidence_ref, image_ref, sems,
 ):
     number = image_ref.shape[0]
     refs = near_ref.shape[0]
     rows_half = FY // 2
     group = 8
+    half = half_ref[0]
+    copies = []
+    for k in range(4):
+        side = half if k < 2 else 1 - half
+        quarter = FY * FX // 2
+        at = pl.ds(pl.multiple_of((side * 2 + k % 2) * quarter, quarter), quarter)
+        copies.append(
+            pltpu.make_async_copy(image_from.at[:, at], image_ref.at[:, at], sems.at[k])
+        )
+        copies[-1].start()
     off_x = offset_ref[:, 0:1]
     off_y = offset_ref[:, 1:2]
     lane = iota((number, FX), 1)
@@ -229,7 +259,7 @@
             axis=0,
         )
 
-    def run(ref, first, total):
+    def run(ref, first, total, waits):
         start_cos, start_sin = wave(-(lane * off_x + first * off_y))
 
         def block(k, carry):
@@ -261,13 +291,16 @@
             )
             return total, cosine, sine
 
-        total, _, _ = lax.fori_loop(0, rows_half // group, block, (total, start_cos, start_sin))
-        return total
-
-    half = half_ref[0]
+        carry = (total, start_cos, start_sin)
+        turns = rows_half // group // len(waits)
+        for k, wait in enumerate(waits):
+            wait.wait()
+            carry = lax.fori_loop(k * turns, (k + 1) * turns, block, carry)
+        return carry[0]
+
     total = jnp.zeros((TY * number, TX * refs), F32)
-    total = run(near_ref, half * rows_half, total)
-    total = run(far_ref, (1 - half) * rows_half, total)
+    total = run(near_ref, half * rows_half, total, copies[:2])
+    total = run(far_ref, (1 - half) * rows_half, total, copies[2:])
     total = total * (1.0 / math.sqrt(FY * 2 * FX))
     parts = [total[b * number : (b + 1) * number, :] for b in range(TY)]
     top = functools.reduce(jnp.maximum, parts)
@@ -297,7 +330,9 @@
     table_ref[...] = table
 
 
-def weights_table(planes, inner, half, images, near, far, offsets, orientations, interp_index):
+def weights_table(
+    planes, inner, half, images, near, far, offsets, orientations, interp_index, token
+):
     number = images.shape[0]
     turn = np.arange(FY) * STEP
     turns = np.stack([np.cos(turn), np.sin(turn), np.cos(2 * turn), np.sin(2 * turn)])
@@ -306,12 +341,14 @@
     return pl.pallas_call(
         functools.partial(score_kernel, planes, inner),
         out_shape=[jax.ShapeDtypeStruct((number, FX), F32)] * 2,
-        in_specs=[smem, smem] + [vmem] * 6,
-        compiler_params=vmem_params(16),
-        cost_estimate=cost(3e9, 5e6),
+        in_specs=[smem, smem, pl.BlockSpec(memory_space=pltpu.HBM)] + [vmem] * 6,
+        scratch_shapes=[pltpu.VMEM(images.shape, BF16), pltpu.SemaphoreType.DMA((4,))],
+        compiler_params=vmem_params(14),
+        cost_estimate=cost(5e9, 5e6),
         name="scores",
     )(
-        half, jnp.asarray(turns, F32), images, near, far, offsets, orientations, interp_index
+        half, jnp.asarray(turns, F32), in_hbm(images), near, far, offsets, orientations,
+        interp_index, token,
     )
 
 
@@ -412,26 +449,24 @@
             value = value + base_ref[at : at + tile, :]
         out_ref[at : at + tile, :] = value
         if first:
-            piece = refs[1 + at // (lines // 2)]
-            spot = at % (lines // 2)
-            piece[spot : spot + tile, :] = value.astype(BF16)
+            refs[1][at : at + tile, :] = value.astype(BF16)
 
 
 def partial_lines(cap, pad, rows, table, mats, lines, first, base=None):
     group = rows.shape[0] // (cap + 16)
     shape = jax.ShapeDtypeStruct((lines, 2 * FX), F32)
-    short = jax.ShapeDtypeStruct((lines // 2, 2 * FX), BF16)
+    short = jax.ShapeDtypeStruct((lines, 2 * FX), BF16)
     vmem = pl.BlockSpec(memory_space=pltpu.VMEM)
     extra = () if base is None else (base,)
     return pl.pallas_call(
         functools.partial(gather_kernel, cap, pad, None if extra else first),
-        out_shape=(shape, short, short) if first else shape,
+        out_shape=(shape, short) if first else shape,
         in_specs=[vmem] * (4 + len(extra)),
         scratch_shapes=[
             pltpu.VMEM((group * cap, 2 * FX), BF16),
             pltpu.VMEM((group, 1, cap), I32),
         ],
-        compiler_params=vmem_params(24),
+        compiler_params=vmem_params(20),
         cost_estimate=cost(1e6, 1e5),
         name="lines",
     )(rows, table, jnp.asarray(wave_table()), mats, *extra)
@@ -476,7 +511,7 @@
         out_shape=[jax.ShapeDtypeStruct(parts[0].shape, BF16)] * 2,
         in_specs=[vmem] * (len(parts) + 2 * len(up)),
         compiler_params=vmem_params(14),
-        cost_estimate=cost(1e6, 1e5),
+        cost_estimate=cost(60e9, 8e6),
         name="relay",
     )(*parts, *up, *down)
 
@@ -514,7 +549,7 @@
 
     place_of = np.argsort(block_order(planes), axis=1).astype(np.int32)
     index, digits, real, imag = row_slots(
-        jnp.asarray(place_of),
+        place_of,
         owners.reshape(number, LIST * FY),
         line_index,
         images,
@@ -530,8 +565,8 @@
     def place(k, index):
         return placed_rows(k, group, cap, index, digits, real, imag)
 
-    early = min(3, planes)
-    placed = [place(k, index) for k in range(early)]
+    first, token = place(0, index)
+    placed = [first]
 
     def to_members(value):
         return lax.all_to_all(
@@ -539,14 +574,15 @@
         ).reshape(group * span, 2 * FX)
 
     got = to_members(placed[0])
-    near, placed[1:3] = together(near, placed[1:3])
+    near, token = together(near, token)
     near = jnp.concatenate(near, axis=0)
     far = lax.ppermute(near, "slab", [(i, i ^ 1) for i in range(slab)])
-    near, far, got = together(near, far, got)
     table, evidence = weights_table(
         planes, inner, half.reshape(1).astype(I32), images, near, far, offsets, orientations,
-        interp_index,
+        interp_index, token,
     )
+    table, got, index = together(table, got, index)
+    placed.append(place(1, index)[0])
     tables = lax.all_to_all(
         jnp.broadcast_to(table[None], (group,) + table.shape), ("x", "slab"), 0, 0, tiled=True
     ).reshape(group * number, FX)
@@ -558,18 +594,14 @@
 
     def fetch(k, value):
         if k < planes:
-            value, placed[k] = together(value, placed[k])
+            value, held = together(value, index)
+            placed.append(place(k, held)[0])
             got.append(to_members(placed[k]))
         return value
 
-    part, *short = lines_of(0)
-    part, index = together(part, index)
-    placed += [place(k, index) for k in range(early, planes)]
-    parts = [part]
-    ends = sorted({(0, 1), (planes - 1, planes - 2)})
-    up = [lax.ppermute(piece, "z", ends) for piece in short]
-    up[0] = fetch(2, up[0])
-    down = up
+    part, short = lines_of(0)
+    parts = [fetch(2, part)]
+    up = down = [lax.ppermute(short, "z", sorted({(0, 1), (planes - 1, planes - 2)}))]
     for s in range(2, planes):
         parts.append(fetch(s + 1, lines_of(s - 1)))
         up_send, down_send = relay(planes, s, place_of, parts, up, down)

time: 205 us -> 189 us (0.922)
  blocking collectives: 9.01 us -> 0 us
  local copies, waits for them, and re-layouts: 15.1 us -> 7.86 us
  starting transfers between devices: 47 us -> 41 us
  Pallas kernels: 102 us -> 107 us
    ppermute x2 -> x1, waiting for transfers between devices: 11.8 us -> 0.01 us  [body(): lax.ppermute(short, 'z', sorted({(0, 1), (planes - 1, planes - 2)}))]
    all_to_all x1 -> x0, blocking collectives: 9.01 us -> none  [body(): lax.all_to_all(jnp.broadcast_to(table[None], (group,) + table.shape), ('x...]
    ppermute x3, waiting for transfers between devices: 0.01 us -> 8.6 us  [body(): lax.ppermute(block, 'z', [(p, (p + shift) % planes) for p in range(planes)])]
    unnamed x46 -> x38, local copies, waits for them, and re-layouts: 14.4 us -> 6.51 us
    ppermute x2, starting transfers between devices: 11.1 us -> 4.65 us  [body(): up = [lax.ppermute(up_send, 'z', [(p, p + 1) for p in range(s)])]]
    all_to_all x4, waiting for transfers between devices: 0.01 us -> 3.81 us  [to_members(): lax.all_to_all(value.reshape(group, span, 2 * FX), ('x', 'slab'), 0, 0, t...]
    all_to_all x0 -> x1, starting transfers between devices: none -> 3.35 us  [body(): lax.all_to_all(jnp.broadcast_to(table[None], (group,) + table.shape), ('x...]
    pallas_call x2, Pallas kernels: 4.5 us -> 6.78 us  [relay(): pl.pallas_call(functools.partial(relay_kernel, planes, step, place_of, le...]
  transfers between devices with their start and end apart: 15 -> 15, of which waited for: 5 -> 5; matrix products, arithmetic and copies ran while one was open for 2% -> 2% of each run, Pallas kernels for 45% -> 57%
where the time goes in v3:
time: 189 us; the launch traced here: 188 us
  Pallas kernels  107 us (57%)
  starting transfers between devices  41 us (22%)
  waiting for transfers between devices  25 us (13%)
  local copies, waits for them, and re-layouts  7.86 us (4%)
  other arithmetic  5.99 us (3%)
    pallas_call x4, Pallas kernels, partial_lines(): pl.pallas_call(functools.partial(gather_kernel, cap, pad, None if extra e...  49.3 us
    pallas_call x4, Pallas kernels, placed_rows(): pl.pallas_call(functools.partial(place_kernel, chunk, cap), grid=(1,), ou...  35.2 us
    all_to_all x4, starting transfers between devices, to_members(): lax.all_to_all(value.reshape(group, span, 2 * FX), ('x', 'slab'), 0, 0, t...  18 us
    pallas_call x1, Pallas kernels, weights_table(): pl.pallas_call(functools.partial(score_kernel, planes, inner), out_shape=...  11.2 us
    ppermute x3, waiting for transfers between devices, body(): lax.ppermute(block, 'z', [(p, (p + shift) % planes) for p in range(planes)])  8.6 us
    pallas_call x2, Pallas kernels, relay(): pl.pallas_call(functools.partial(relay_kernel, planes, step, place_of, le...  6.78 us
    unnamed x38, local copies, waits for them, and re-layouts  6.51 us
    ppermute x2, waiting for transfers between devices, body(): lax.ppermute(down_send, 'z', [(p, p - 1) for p in range(planes - s, plane...  5.18 us
  transfers between devices with their start and end apart: 15, of which 5 were waited for; matrix products, arithmetic and copies ran while one was open for 2% of the time, Pallas kernels for 57%

profile of v3, /device:TPU:0, one launch (start us, length us, event | category | flops | bytes accessed | tf_op | source)
XLA Modules:
  0.0 188.1 jit_solution(14447110438275841929)
XLA Ops:
  1.7 3.0 %collective-permute-start = (bf16[2,32768]{1,0:T(2,128)(2,1)S(1)}, bf16[2,32768]{1,0:T(2,128)(2,1)S(1)}, u32[]{:S(2)}, u32[]{:S(2)}) collective-permute-start(bf16[2,32768]{1,0:T(2,128)(2,1)S(1)} %constant_dynamic-slice_fusion), channel_id=1, source_target_pairs={{0,4},{4,0},{1,5},{5,1},{2,6},{6,2},{3,7},{7,3},{8,12},{12,8},{9,1... | collective-permute-start | bytes 393224 | tf_op jit(solution)/shard_map/ppermute | solution.py:548
  5.4 4.7 %slots.1 = (s32[32,512]{1,0:T(8,128)S(1)}, f32[128,512]{1,0:T(8,128)S(1)}, f32[4096,128]{1,0:T(8,128)S(1)}, f32[4096,128]{1,0:T(8,128)S(1)}) custom-call(s32[16,512]{1,0:T(8,128)S(1)} %bitcast.18, s32[16,512]{1,0:T(8,128)} %line_from.1, bf16[16,65536]{1,0:T(8,128)(2,1)} %image_from.3), custom_call_target="tpu_custom_call" | custom-call | flops 3000000000 | bytes 12000000 | tf_op jit(solution)/shard_map/slots/pallas_call | solution.py:123
  10.4 3.6 %collective-permute-start.3 = (bf16[4,32768]{1,0:T(4,128)(2,1)S(1)}, bf16[4,32768]{1,0:T(4,128)(2,1)S(1)}, u32[]{:S(2)}, u32[]{:S(2)}) collective-permute-start(bf16[4,32768]{1,0:T(4,128)(2,1)S(1)} %pad_maximum_fusion.1), channel_id=1, source_target_pairs={{0,24},{8,0},{16,8},{24,16},{1,25},{9,1},{17,9},{25,17},{2,26},{10... | collective-permute-start | bytes 786440 | tf_op jit(solution)/shard_map/ppermute | solution.py:564
  15.1 7.9 %place.4 = (bf16[3712,256]{1,0:T(8,128)(2,1)}, f32[8,128]{1,0:T(8,128)S(1)}) custom-call(s32[32,512]{1,0:T(8,128)S(1)} %get-tuple-element.56.index_ref, f32[128,512]{1,0:T(8,128)S(1)} %get-tuple-element.40.digit_ref, f32[4096,128]{1,0:T(8,128)S(1)} %get-tuple-element.41.real_ref, f32[4096,128]{1,0:T(8,128)S(1)} %get-tuple-element.42.imag_ref), custom_call_target="tpu_custom_call" | custom-call | flops 100000 | bytes 100000 | tf_op jit(solution)/shard_map/place/pallas_call | solution.py:191
  23.0 4.5 %all-to-all-start = ((bf16[8,464,256]{2,1,0:T(8,128)(2,1)}), bf16[8,464,256]{2,1,0:T(8,128)(2,1)}, u32[]{:S(2)}, u32[]{:S(2)}) async-start(bf16[8,464,256]{2,1,0:T(8,128)(2,1)} %bitcast.20), calls=%async_computation | async-start | bytes 3801088 | tf_op jit(solution)/shard_map/all_to_all | solution.py:572
  27.5 8.6 %collective-permute-done.2 = bf16[4,32768]{1,0:T(4,128)(2,1)S(1)} collective-permute-done((bf16[4,32768]{1,0:T(4,128)(2,1)S(1)}, bf16[4,32768]{1,0:T(4,128)(2,1)S(1)}, u32[]{:S(2)}, u32[]{:S(2)}) %collective-permute-start.2) | collective-permute-done | bytes 262176 | tf_op jit(solution)/shard_map/ppermute | solution.py:564
  36.1 2.6 %pad_maximum_fusion.near_ref = bf16[16,32768]{1,0:T(8,128)(2,1)} fusion(bf16[4,32768]{1,0:T(4,128)(2,1)S(1)} %collective-permute-done.3, bf16[4,32768]{1,0:T(4,128)(2,1)S(1)} %collective-permute-done.2, bf16[4,32768]{1,0:T(4,128)(2,1)} %collective-permute-done.1, bf16[4,32768]{1,0:T(4,128)(2,1)S(1)} %pad_maximum_fusion.1), kind=kLoop, calls=%fused_computation.1 | loop fusion | flops 4194304 | bytes 2097152 | tf_op jit(solution)/shard_map/concatenate | solution.py:578
  39.0 2.7 %collective-permute-done.4.far_ref = bf16[16,32768]{1,0:T(8,128)(2,1)} collective-permute-done((bf16[16,32768]{1,0:T(8,128)(2,1)}, bf16[16,32768]{1,0:T(8,128)(2,1)}, u32[]{:S(2)}, u32[]{:S(2)}) %collective-permute-start.4) | collective-permute-done | bytes 1048608 | tf_op jit(solution)/shard_map/ppermute | solution.py:579
  41.7 11.2 %scores.1 = (f32[16,128]{1,0:T(8,128)S(1)}, f32[16,128]{1,0:T(8,128)S(1)}) custom-call(s32[1]{0:T(128)} %bitcast.half_ref, f32[4,256]{1,0:T(4,128)S(1)} %copy-done.13, bf16[16,65536]{1,0:T(8,128)(2,1)} %image_from.3, bf16[16,32768]{1,0:T(8,128)(2,1)} %pad_maximum_fusion.near_ref, bf16[16,32768]{1,0:T(8,128)(2,1)} %collective-permute-done.4.far_ref, ...), custom_call_target="tpu_custom_call" | custom-call | flops 5000000000 | bytes 5000000 | tf_op jit(solution)/shard_map/scores/pallas_call | solution.py:341
  53.6 3.4 %all-to-all-start.1 = ((f32[8,16,128]{2,1,0:T(8,128)}), f32[8,16,128]{2,1,0:T(8,128)S(1)}, u32[]{:S(2)}, u32[]{:S(2)}) async-start(f32[8,16,128]{2,1,0:T(8,128)} %broadcast_in_dim.2), calls=%async_computation.1 | async-start | bytes 131072 | tf_op jit(solution)/shard_map/all_to_all | solution.py:586
  57.0 1.6 copy-done.2
  58.5 8.8 %place.5 = (bf16[3712,256]{1,0:T(8,128)(2,1)}, f32[8,128]{1,0:T(8,128)}) custom-call(s32[32,512]{1,0:T(8,128)S(1)} %get-tuple-element.56.index_ref, f32[128,512]{1,0:T(8,128)S(1)} %get-tuple-element.40.digit_ref, f32[4096,128]{1,0:T(8,128)S(1)} %get-tuple-element.41.real_ref, f32[4096,128]{1,0:T(8,128)S(1)} %copy-done.2), custom_call_target="tpu_custom_call" | custom-call | flops 100000 | bytes 100000 | tf_op jit(solution)/shard_map/place/pallas_call | solution.py:191
  67.3 5.3 %all-to-all-start.2 = ((bf16[8,464,256]{2,1,0:T(8,128)(2,1)}), bf16[8,464,256]{2,1,0:T(8,128)(2,1)}, u32[]{:S(2)}, u32[]{:S(2)}) async-start(bf16[8,464,256]{2,1,0:T(8,128)(2,1)} %bitcast.22), calls=%async_computation.2 | async-start | bytes 3801088 | tf_op jit(solution)/shard_map/all_to_all | solution.py:572
  72.6 13.5 %lines.6 = (f32[2048,256]{1,0:T(8,128)S(1)}, bf16[2048,256]{1,0:T(8,128)(2,1)}) custom-call(bf16[3712,256]{1,0:T(8,128)(2,1)} %bitcast.2.row_ref, f32[128,128]{1,0:T(8,128)S(1)} %bitcast.14, bf16[144,256]{1,0:T(8,128)(2,1)S(1)} %copy-done.9, bf16[8,128,128]{2,1,0:T(8,128)(2,1)S(1)} %copy-done.5), custom_call_target="tpu_custom_call" | custom-call | flops 1000000 | bytes 100000 | tf_op jit(solution)/shard_map/lines/pallas_call | solution.py:461
  87.5 4.4 %collective-permute-start.5 = (bf16[2048,256]{1,0:T(8,128)(2,1)}, bf16[2048,256]{1,0:T(8,128)(2,1)}, u32[]{:S(2)}, u32[]{:S(2)}) collective-permute-start(bf16[2048,256]{1,0:T(8,128)(2,1)} %get-tuple-element.64), channel_id=1, source_target_pairs={{0,8},{24,16},{1,9},{25,17},{2,10},{26,18},{3,11},{27,19},{4,12},{... | collective-permute-start | bytes 3145736 | tf_op jit(solution)/shard_map/ppermute | solution.py:604
  91.9 8.8 %place.7 = (bf16[3712,256]{1,0:T(8,128)(2,1)}, f32[8,128]{1,0:T(8,128)}) custom-call(s32[32,512]{1,0:T(8,128)S(1)} %get-tuple-element.56.index_ref, f32[128,512]{1,0:T(8,128)S(1)} %get-tuple-element.40.digit_ref, f32[4096,128]{1,0:T(8,128)S(1)} %get-tuple-element.41.real_ref, f32[4096,128]{1,0:T(8,128)S(1)} %copy-done.3), custom_call_target="tpu_custom_call" | custom-call | flops 100000 | bytes 100000 | tf_op jit(solution)/shard_map/place/pallas_call | solution.py:191
  100.8 4.3 %all-to-all-start.4 = ((bf16[8,464,256]{2,1,0:T(8,128)(2,1)}), bf16[8,464,256]{2,1,0:T(8,128)(2,1)}, u32[]{:S(2)}, u32[]{:S(2)}) async-start(bf16[8,464,256]{2,1,0:T(8,128)(2,1)} %bitcast.21), calls=%async_computation.4 | async-start | bytes 3801088 | tf_op jit(solution)/shard_map/all_to_all | solution.py:572
  105.1 12.5 %lines.4.refs_1_ = f32[2048,256]{1,0:T(8,128)S(1)} custom-call(bf16[3712,256]{1,0:T(8,128)(2,1)} %bitcast.5.row_ref, f32[128,128]{1,0:T(8,128)S(1)} %bitcast.15, bf16[144,256]{1,0:T(8,128)(2,1)S(1)} %copy-done.9, bf16[8,128,128]{2,1,0:T(8,128)(2,1)S(1)} %copy-done.5), custom_call_target="tpu_custom_call" | custom-call | flops 1000000 | bytes 100000 | tf_op jit(solution)/shard_map/lines/pallas_call | solution.py:461
  117.7 3.8 %relay.2 = (bf16[2048,256]{1,0:T(8,128)(2,1)}, bf16[2048,256]{1,0:T(8,128)(2,1)}) custom-call(f32[2048,256]{1,0:T(8,128)S(1)} %copy-done.11, f32[2048,256]{1,0:T(8,128)S(1)} %lines.4.refs_1_, bf16[2048,256]{1,0:T(8,128)(2,1)} %collective-permute-done.5.refs_2_.refs_3_, bf16[2048,256]{1,0:T(8,128)(2,1)} %collective-permute-done.5.refs_2_.refs_3_), custom_call_target="tpu_custom_call" | custom-call | flops 60000002048 | bytes 8000000 | tf_op jit(solution)/shard_map/relay/pallas_call | solution.py:509
  121.4 2.3 %collective-permute-start.6 = (bf16[2048,256]{1,0:T(8,128)(2,1)}, bf16[2048,256]{1,0:T(8,128)(2,1)}, u32[]{:S(2)}, u32[]{:S(2)}) collective-permute-start(bf16[2048,256]{1,0:T(8,128)(2,1)} %get-tuple-element.65), channel_id=1, source_target_pairs={{0,8},{8,16},{1,9},{9,17},{2,10},{10,18},{3,11},{11,19},{4,12},{12... | collective-permute-start | bytes 3145736 | tf_op jit(solution)/shard_map/ppermute | solution.py:608
  123.8 1.6 collective-permute-start.7
  125.4 9.7 %place.6 = (bf16[3712,256]{1,0:T(8,128)(2,1)}, f32[8,128]{1,0:T(8,128)}) custom-call(s32[32,512]{1,0:T(8,128)S(1)} %get-tuple-element.56.index_ref, f32[128,512]{1,0:T(8,128)S(1)} %get-tuple-element.40.digit_ref, f32[4096,128]{1,0:T(8,128)S(1)} %get-tuple-element.41.real_ref, f32[4096,128]{1,0:T(8,128)S(1)} %copy-done.4), custom_call_target="tpu_custom_call" | custom-call | flops 100000 | bytes 100000 | tf_op jit(solution)/shard_map/place/pallas_call | solution.py:191
  135.2 3.9 %all-to-all-start.3 = ((bf16[8,464,256]{2,1,0:T(8,128)(2,1)}), bf16[8,464,256]{2,1,0:T(8,128)(2,1)S(1)}, u32[]{:S(2)}, u32[]{:S(2)}) async-start(bf16[8,464,256]{2,1,0:T(8,128)(2,1)} %bitcast.19), calls=%async_computation.3 | async-start | bytes 3801088 | tf_op jit(solution)/shard_map/all_to_all | solution.py:572
  139.1 12.5 %lines.7.refs_2_ = f32[2048,256]{1,0:T(8,128)S(1)} custom-call(bf16[3712,256]{1,0:T(8,128)(2,1)} %bitcast.9.row_ref, f32[128,128]{1,0:T(8,128)S(1)} %bitcast.16, bf16[144,256]{1,0:T(8,128)(2,1)S(1)} %copy-done.9, bf16[8,128,128]{2,1,0:T(8,128)(2,1)S(1)} %copy-done.5), custom_call_target="tpu_custom_call" | custom-call | flops 1000000 | bytes 100000 | tf_op jit(solution)/shard_map/lines/pallas_call | solution.py:461
  151.6 3.0 %relay.3 = (bf16[2048,256]{1,0:T(8,128)(2,1)}, bf16[2048,256]{1,0:T(8,128)(2,1)}) custom-call(f32[2048,256]{1,0:T(8,128)S(1)} %copy-done.12, f32[2048,256]{1,0:T(8,128)S(1)} %copy-done.8, f32[2048,256]{1,0:T(8,128)S(1)} %lines.7.refs_2_, bf16[2048,256]{1,0:T(8,128)(2,1)} %collective-permute-done.6.refs_3_, bf16[2048,256]{1,0:T(8,128)(2,1)} %collective-permute-done.7.refs_4_), custom_call_target="tpu_custom_call" | custom-call | flops 60000002048 | bytes 8000000 | tf_op jit(solution)/shard_map/relay/pallas_call | solution.py:509
  154.6 2.3 %collective-permute-start.8 = (bf16[2048,256]{1,0:T(8,128)(2,1)}, bf16[2048,256]{1,0:T(8,128)(2,1)}, u32[]{:S(2)}, u32[]{:S(2)}) collective-permute-start(bf16[2048,256]{1,0:T(8,128)(2,1)} %get-tuple-element.67), channel_id=1, source_target_pairs={{0,8},{8,16},{16,24},{1,9},{9,17},{17,25},{2,10},{10,18},{18,26},{... | collective-permute-start | bytes 3145736 | tf_op jit(solution)/shard_map/ppermute | solution.py:608
  158.9 3.8 %all-to-all-done.3 = bf16[8,464,256]{2,1,0:T(8,128)(2,1)S(1)} async-done(((bf16[8,464,256]{2,1,0:T(8,128)(2,1)}), bf16[8,464,256]{2,1,0:T(8,128)(2,1)S(1)}, u32[]{:S(2)}, u32[]{:S(2)}) %all-to-all-start.3) | async-done | bytes 1900576 | tf_op jit(solution)/shard_map/all_to_all | solution.py:572
  162.7 1.6 copy-done.6
  164.3 10.8 %lines.5 = f32[2048,256]{1,0:T(8,128)S(1)} custom-call(bf16[3712,256]{1,0:T(8,128)(2,1)S(1)} %bitcast.13, f32[128,128]{1,0:T(8,128)S(1)} %bitcast.17, bf16[144,256]{1,0:T(8,128)(2,1)S(1)} %copy-done.9, bf16[8,128,128]{2,1,0:T(8,128)(2,1)S(1)} %copy-done.5, f32[2048,256]{1,0:T(8,128)S(1)} %copy-done.6), custom_call_target="tpu_custom_call" | custom-call | flops 1000000 | bytes 100000 | tf_op jit(solution)/shard_map/lines/pallas_call | solution.py:461
  175.1 4.7 %collective-permute-done.8 = bf16[2048,256]{1,0:T(8,128)(2,1)} collective-permute-done((bf16[2048,256]{1,0:T(8,128)(2,1)}, bf16[2048,256]{1,0:T(8,128)(2,1)}, u32[]{:S(2)}, u32[]{:S(2)}) %collective-permute-start.8) | collective-permute-done | bytes 1048608 | tf_op jit(solution)/shard_map/ppermute | solution.py:608
  179.8 5.2 %collective-permute-done.9 = bf16[2048,256]{1,0:T(8,128)(2,1)} collective-permute-done((bf16[2048,256]{1,0:T(8,128)(2,1)}, bf16[2048,256]{1,0:T(8,128)(2,1)}, u32[]{:S(2)}, u32[]{:S(2)}) %collective-permute-start.9) | collective-permute-done | bytes 1048608 | tf_op jit(solution)/shard_map/ppermute | solution.py:609
  184.9 3.1 %convert_add_fusion = f32[2048,256]{1,0:T(8,128)} fusion(bf16[2048,256]{1,0:T(8,128)(2,1)} %collective-permute-done.9, f32[2048,256]{1,0:T(8,128)S(1)} %lines.5, bf16[2048,256]{1,0:T(8,128)(2,1)} %collective-permute-done.8), kind=kLoop, calls=%fused_computation | loop fusion | flops 2097152 | bytes 6291456 | tf_op jit(solution)/shard_map/add | solution.py:611
  (54 shorter events, 7.3 us)
Async XLA Ops:
  0.6 1.0 copy-start
  1.7 8.5 %collective-permute-start = (bf16[2,32768]{1,0:T(2,128)(2,1)S(1)}, bf16[2,32768]{1,0:T(2,128)(2,1)S(1)}, u32[]{:S(2)}, u32[]{:S(2)}) collective-permute-start(bf16[2,32768]{1,0:T(2,128)(2,1)S(1)} %constant_dynamic-slice_fusion), channel_id=1, source_target_pairs={{0,4},{4,0},{1,5},{5,1},{2,6},{6,2},{3,7},{7,3},{8,12},{12,8},{9,1... | collective-permute-start | bytes 393224 | tf_op jit(solution)/shard_map/ppermute | solution.py:548
  10.1 12.8 %copy-start.1 = (f32[4096,128]{1,0:T(8,128)}, f32[4096,128]{1,0:T(8,128)S(1)}, u32[]{:S(2)}) copy-start(f32[4096,128]{1,0:T(8,128)S(1)} %get-tuple-element.42.imag_ref) | copy-start | bytes 6291460
  10.4 17.1 %collective-permute-start.3 = (bf16[4,32768]{1,0:T(4,128)(2,1)S(1)}, bf16[4,32768]{1,0:T(4,128)(2,1)S(1)}, u32[]{:S(2)}, u32[]{:S(2)}) collective-permute-start(bf16[4,32768]{1,0:T(4,128)(2,1)S(1)} %pad_maximum_fusion.1), channel_id=1, source_target_pairs={{0,24},{8,0},{16,8},{24,16},{1,25},{9,1},{17,9},{25,17},{2,26},{10... | collective-permute-start | bytes 786440 | tf_op jit(solution)/shard_map/ppermute | solution.py:564
  14.1 22.0 %collective-permute-start.2 = (bf16[4,32768]{1,0:T(4,128)(2,1)S(1)}, bf16[4,32768]{1,0:T(4,128)(2,1)S(1)}, u32[]{:S(2)}, u32[]{:S(2)}) collective-permute-start(bf16[4,32768]{1,0:T(4,128)(2,1)S(1)} %pad_maximum_fusion.1), channel_id=1, source_target_pairs={{0,16},{8,24},{16,0},{24,8},{1,17},{9,25},{17,1},{25,9},{2,18},{10... | collective-permute-start | bytes 786440 | tf_op jit(solution)/shard_map/ppermute | solution.py:564
  14.1 22.0 %collective-permute-start.1 = (bf16[4,32768]{1,0:T(4,128)(2,1)S(1)}, bf16[4,32768]{1,0:T(4,128)(2,1)}, u32[]{:S(2)}, u32[]{:S(2)}) collective-permute-start(bf16[4,32768]{1,0:T(4,128)(2,1)S(1)} %pad_maximum_fusion.1), channel_id=1, source_target_pairs={{0,8},{8,16},{16,24},{24,0},{1,9},{9,17},{17,25},{25,1},{2,10},{10... | collective-permute-start | bytes 786440 | tf_op jit(solution)/shard_map/ppermute | solution.py:564
  23.0 15.7 %copy-start.14 = (s32[16,2]{0,1:T(2,128)S(1)}, s32[16,2]{0,1:T(2,128)}, u32[]{:S(2)}) copy-start(s32[16,2]{0,1:T(2,128)} %param.16) | copy-start | bytes 388
  23.0 15.8 %copy-start.15 = (s32[16,2]{0,1:T(2,128)S(1)}, s32[16,2]{0,1:T(2,128)}, u32[]{:S(2)}) copy-start(s32[16,2]{0,1:T(2,128)} %param.17) | copy-start | bytes 388
  23.0 15.9 %copy-start.16 = (s32[16,2]{0,1:T(2,128)S(1)}, s32[16,2]{0,1:T(2,128)}, u32[]{:S(2)}) copy-start(s32[16,2]{0,1:T(2,128)} %param.19) | copy-start | bytes 388
  23.0 18.7 %copy-start.13 = (f32[4,256]{1,0:T(4,128)S(1)}, f32[4,256]{1,0:T(4,128)}, u32[]{:S(2)}) copy-start(f32[4,256]{1,0:T(4,128)} %constant.26.clone.turn_ref) | copy-start | bytes 12292
  23.0 29.9 %all-to-all-start = ((bf16[8,464,256]{2,1,0:T(8,128)(2,1)}), bf16[8,464,256]{2,1,0:T(8,128)(2,1)}, u32[]{:S(2)}, u32[]{:S(2)}) async-start(bf16[8,464,256]{2,1,0:T(8,128)(2,1)} %bitcast.20), calls=%async_computation | async-start | bytes 3801088 | tf_op jit(solution)/shard_map/all_to_all | solution.py:572
  38.7 3.0 %collective-permute-start.4 = (bf16[16,32768]{1,0:T(8,128)(2,1)}, bf16[16,32768]{1,0:T(8,128)(2,1)}, u32[]{:S(2)}, u32[]{:S(2)}) collective-permute-start(bf16[16,32768]{1,0:T(8,128)(2,1)} %pad_maximum_fusion.near_ref), channel_id=1, source_target_pairs={{0,1},{1,0},{2,3},{3,2},{4,5},{5,4},{6,7},{7,6},{8,9},{9,8},{10,11... | collective-permute-start | bytes 3145736 | tf_op jit(solution)/shard_map/ppermute | solution.py:579
  53.6 13.7 %all-to-all-start.1 = ((f32[8,16,128]{2,1,0:T(8,128)}), f32[8,16,128]{2,1,0:T(8,128)S(1)}, u32[]{:S(2)}, u32[]{:S(2)}) async-start(f32[8,16,128]{2,1,0:T(8,128)} %broadcast_in_dim.2), calls=%async_computation.1 | async-start | bytes 131072 | tf_op jit(solution)/shard_map/all_to_all | solution.py:586
  57.0 1.6 copy-start.2
  67.3 5.3 %copy-start.5 = (bf16[8,128,128]{2,1,0:T(8,128)(2,1)S(1)}, bf16[8,128,128]{2,1,0:T(8,128)(2,1)}, u32[]{:S(2)}) copy-start(bf16[8,128,128]{2,1,0:T(8,128)(2,1)} %mats_ref.7) | copy-start | bytes 786436
  67.3 5.3 %copy-start.9 = (bf16[144,256]{1,0:T(8,128)(2,1)S(1)}, bf16[144,256]{1,0:T(8,128)(2,1)}, u32[]{:S(2)}) copy-start(bf16[144,256]{1,0:T(8,128)(2,1)} %constant.27.clone.wave_ref) | copy-start | bytes 221188
  67.3 33.4 %all-to-all-start.2 = ((bf16[8,464,256]{2,1,0:T(8,128)(2,1)}), bf16[8,464,256]{2,1,0:T(8,128)(2,1)}, u32[]{:S(2)}, u32[]{:S(2)}) async-start(bf16[8,464,256]{2,1,0:T(8,128)(2,1)} %bitcast.22), calls=%async_computation.2 | async-start | bytes 3801088 | tf_op jit(solution)/shard_map/all_to_all | solution.py:572
  72.6 19.3 %copy-start.3 = (f32[4096,128]{1,0:T(8,128)S(1)}, f32[4096,128]{1,0:T(8,128)}, u32[]{:S(2)}) copy-start(f32[4096,128]{1,0:T(8,128)} %copy-done.1) | copy-start | bytes 6291460
  86.1 1.3 copy-start.10
  87.5 30.2 %collective-permute-start.5 = (bf16[2048,256]{1,0:T(8,128)(2,1)}, bf16[2048,256]{1,0:T(8,128)(2,1)}, u32[]{:S(2)}, u32[]{:S(2)}) collective-permute-start(bf16[2048,256]{1,0:T(8,128)(2,1)} %get-tuple-element.64), channel_id=1, source_target_pairs={{0,8},{24,16},{1,9},{25,17},{2,10},{26,18},{3,11},{27,19},{4,12},{... | collective-permute-start | bytes 3145736 | tf_op jit(solution)/shard_map/ppermute | solution.py:604
  100.8 34.4 %all-to-all-start.4 = ((bf16[8,464,256]{2,1,0:T(8,128)(2,1)}), bf16[8,464,256]{2,1,0:T(8,128)(2,1)}, u32[]{:S(2)}, u32[]{:S(2)}) async-start(bf16[8,464,256]{2,1,0:T(8,128)(2,1)} %bitcast.21), calls=%async_computation.4 | async-start | bytes 3801088 | tf_op jit(solution)/shard_map/all_to_all | solution.py:572
  105.1 12.6 %copy-start.11 = (f32[2048,256]{1,0:T(8,128)S(1)}, f32[2048,256]{1,0:T(8,128)}, u32[]{:S(2)}) copy-start(f32[2048,256]{1,0:T(8,128)} %copy-done.10) | copy-start | bytes 6291460
  117.6 3.8 %copy-start.7 = (f32[2048,256]{1,0:T(8,128)}, f32[2048,256]{1,0:T(8,128)S(1)}, u32[]{:S(2)}) copy-start(f32[2048,256]{1,0:T(8,128)S(1)} %lines.4.refs_1_) | copy-start | bytes 6291460
  117.6 7.8 %copy-start.4 = (f32[4096,128]{1,0:T(8,128)S(1)}, f32[4096,128]{1,0:T(8,128)}, u32[]{:S(2)}) copy-start(f32[4096,128]{1,0:T(8,128)} %copy-done.1) | copy-start | bytes 6291460
  121.4 30.2 %collective-permute-start.6 = (bf16[2048,256]{1,0:T(8,128)(2,1)}, bf16[2048,256]{1,0:T(8,128)(2,1)}, u32[]{:S(2)}, u32[]{:S(2)}) collective-permute-start(bf16[2048,256]{1,0:T(8,128)(2,1)} %get-tuple-element.65), channel_id=1, source_target_pairs={{0,8},{8,16},{1,9},{9,17},{2,10},{10,18},{3,11},{11,19},{4,12},{12... | collective-permute-start | bytes 3145736 | tf_op jit(solution)/shard_map/ppermute | solution.py:608
  123.8 27.8 %collective-permute-start.7 = (bf16[2048,256]{1,0:T(8,128)(2,1)}, bf16[2048,256]{1,0:T(8,128)(2,1)}, u32[]{:S(2)}, u32[]{:S(2)}) collective-permute-start(bf16[2048,256]{1,0:T(8,128)(2,1)} %get-tuple-element.66), channel_id=1, source_target_pairs={{16,8},{24,16},{17,9},{25,17},{18,10},{26,18},{19,11},{27,19},{20,... | collective-permute-start | bytes 3145736 | tf_op jit(solution)/shard_map/ppermute | solution.py:609
  135.2 27.5 %all-to-all-start.3 = ((bf16[8,464,256]{2,1,0:T(8,128)(2,1)}), bf16[8,464,256]{2,1,0:T(8,128)(2,1)S(1)}, u32[]{:S(2)}, u32[]{:S(2)}) async-start(bf16[8,464,256]{2,1,0:T(8,128)(2,1)} %bitcast.19), calls=%async_computation.3 | async-start | bytes 3801088 | tf_op jit(solution)/shard_map/all_to_all | solution.py:572
  139.1 12.6 %copy-start.8 = (f32[2048,256]{1,0:T(8,128)S(1)}, f32[2048,256]{1,0:T(8,128)}, u32[]{:S(2)}) copy-start(f32[2048,256]{1,0:T(8,128)} %copy-done.7) | copy-start | bytes 6291460
  139.1 12.6 %copy-start.12 = (f32[2048,256]{1,0:T(8,128)S(1)}, f32[2048,256]{1,0:T(8,128)}, u32[]{:S(2)}) copy-start(f32[2048,256]{1,0:T(8,128)} %copy-done.10) | copy-start | bytes 6291460
  154.6 25.1 %collective-permute-start.8 = (bf16[2048,256]{1,0:T(8,128)(2,1)}, bf16[2048,256]{1,0:T(8,128)(2,1)}, u32[]{:S(2)}, u32[]{:S(2)}) collective-permute-start(bf16[2048,256]{1,0:T(8,128)(2,1)} %get-tuple-element.67), channel_id=1, source_target_pairs={{0,8},{8,16},{16,24},{1,9},{9,17},{17,25},{2,10},{10,18},{18,26},{... | collective-permute-start | bytes 3145736 | tf_op jit(solution)/shard_map/ppermute | solution.py:608
  157.0 28.0 %collective-permute-start.9 = (bf16[2048,256]{1,0:T(8,128)(2,1)}, bf16[2048,256]{1,0:T(8,128)(2,1)}, u32[]{:S(2)}, u32[]{:S(2)}) collective-permute-start(bf16[2048,256]{1,0:T(8,128)(2,1)} %get-tuple-element.68), channel_id=1, source_target_pairs={{8,0},{16,8},{24,16},{9,1},{17,9},{25,17},{10,2},{18,10},{26,18},{... | collective-permute-start | bytes 3145736 | tf_op jit(solution)/shard_map/ppermute | solution.py:609
  162.7 1.6 copy-start.6
